TPU v7x, 256 devices: a whole 4x4x8 slice. The times are simulated.
256 devices in a mesh: grp: 8 (over y, x_lo), node: 32 (over x_hi, z, core).
Axes of the slice: x: 4 (x_hi: 2, x_lo: 2; x = x_hi * 2 + x_lo), y: 4, z: 8, core: 2. Of those that a mesh axis runs over, the one named last changes fastest.
Arguments:
- coefficients: float32 [65536, 1024], P(('grp', 'node')), may hold values from -6 to 6
- transfer: float32 [8, 65536, 512], P(None, ('grp', 'node')), may hold values from -0.3125 to 0.3125
- ranks: int32 [8, 256], P(None, ('grp', 'node')), may hold values from 128 to 256, as said below
Outputs:
- applied: float32 [65536, 1024], P(('grp', 'node'))
Inputs may be any that keep to these rules, and one draw needn't show every extreme that they name: `ranks`: in each level some block has rank exactly 256 and some block rank 256 // 2.
All inputs are finite; a program needn't handle non-finite values.
Results may differ from a plain program's by a relative error of at most 0.00011.
Values sent between devices are 32-bit elements; how exact they have to be, the bound alone decides.
No kernel may reach another device: no remote copies, remote signals or barrier semaphores. Data moves between devices by JAX's collectives and lax.ppermute only.
A program may use at most 128 MiB of HBM per device.

v0:
```python
import jax
import jax.numpy as jnp
from jax import lax
from jax.sharding import PartitionSpec as P


def from_partner(x, axis, stride):
    return lax.ppermute(x, axis, [(i, i ^ 1 << stride) for i in range(lax.axis_size(axis))])


def apply_level(current, matrix, limit, upper_half, mover):
    width = current.shape[0]
    own_cols = lax.dynamic_slice_in_dim(matrix, upper_half * width, width, 1)
    first_term = jnp.dot(
        own_cols, current, precision=lax.Precision.HIGHEST, preferred_element_type=jnp.float32
    )
    partner = mover(current)
    other_cols = lax.dynamic_slice_in_dim(matrix, (1 - upper_half) * width, width, 1)
    mixed = first_term + jnp.dot(
        other_cols, partner, precision=lax.Precision.HIGHEST, preferred_element_type=jnp.float32
    )
    row_ids = jnp.arange(width, dtype=jnp.int32)
    return jnp.where((row_ids < limit)[:, None], mixed, jnp.zeros_like(mixed))


def per_device(coefficients, transfer, ranks):
    node_bits = lax.axis_size("node").bit_length() - 1
    group_bits = lax.axis_size("grp").bit_length() - 1
    node_place = lax.axis_index("node")
    group_place = lax.axis_index("grp")
    current = coefficients
    for level_bit in range(node_bits):

        def node_move(values, bit_number=level_bit):
            return from_partner(values, "node", bit_number)

        upper_half = node_place >> level_bit & 1
        current = apply_level(
            current, transfer[level_bit], ranks[level_bit, 0], upper_half, node_move
        )
    for level_bit in range(group_bits):

        def group_move(values, bit_number=level_bit):
            return from_partner(values, "grp", bit_number)

        level = node_bits + level_bit
        upper_half = group_place >> level_bit & 1
        current = apply_level(current, transfer[level], ranks[level, 0], upper_half, group_move)
    return current


def solution(mesh):
    return jax.shard_map(
        per_device,
        mesh=mesh,
        in_specs=(
            P(("grp", "node"), None),
            P(None, ("grp", "node"), None),
            P(None, ("grp", "node")),
        ),
        out_specs=P(("grp", "node"), None),
        check_vma=False,
    )
```

profile of v0, /device:TPU:8, one launch (start us, length us, event | category | flops | bytes accessed | tf_op | source)
XLA Modules:
  0.0 247.9 jit_solution(17613789358153301384)
XLA Ops:
  0.0 0.0 collective-permute-start
  0.0 1.6 fusion.65
  1.6 0.7 iota_compare_fusion
  2.3 0.0 copy-start
  2.3 3.8 %fusion.64 = (f32[1,256,512]{2,1,0:T(8,128)S(1)}, f32[1,256,512]{2,1,0:T(8,128)}, f32[1,256,512]{2,1,0:T(8,128)}, f32[1,256,512]{2,1,0:T(8,128)S(1)}, f32[1,256,...) fusion(f32[8,256,512]{2,1,0:T(8,128)} %param.4), kind=kLoop, calls=%fused_computation.80 | loop fusion | bytes 8388608 | tf_op jit(solution)/shard_map/slice | solution.py:48
  6.1 0.0 copy-done
  6.1 1.0 fusion.16
  7.1 0.0 collective-permute-done
  7.1 2.3 fusion.7
  9.4 2.0 collective-permute-start.1
  11.4 0.6 iota_compare_fusion.1
  12.0 2.0 fusion.18
  14.0 21.3 %collective-permute-done.1 = f32[256,1024]{1,0:T(8,128)} collective-permute-done((f32[256,1024]{1,0:T(8,128)S(1)}, f32[256,1024]{1,0:T(8,128)}, u32[]{:S(2)}, u32[]{:S(2)}) %collective-permute-start.1) | collective-permute-done | bytes 1048608 | tf_op jit(solution)/shard_map/ppermute | solution.py:8
  35.3 2.4 fusion.6
  37.7 3.4 %collective-permute-start.2 = (f32[256,1024]{1,0:T(8,128)S(1)}, f32[256,1024]{1,0:T(8,128)}, u32[]{:S(2)}, u32[]{:S(2)}) collective-permute-start(f32[256,1024]{1,0:T(8,128)S(1)} %fusion.6), channel_id=1, source_target_pairs={{0,4},{1,5},{2,6},{3,7},{4,0},{5,1},{6,2},{7,3},{8,12},{9,13},{10,... | collective-permute-start | bytes 3145736 | tf_op jit(solution)/shard_map/ppermute | solution.py:8
  41.1 0.6 iota_compare_fusion.2
  41.6 2.0 fusion.20
  43.6 43.2 %collective-permute-done.2 = f32[256,1024]{1,0:T(8,128)} collective-permute-done((f32[256,1024]{1,0:T(8,128)S(1)}, f32[256,1024]{1,0:T(8,128)}, u32[]{:S(2)}, u32[]{:S(2)}) %collective-permute-start.2) | collective-permute-done | bytes 1048608 | tf_op jit(solution)/shard_map/ppermute | solution.py:8
  86.8 2.4 fusion.5
  89.2 6.4 %collective-permute-start.3 = (f32[256,1024]{1,0:T(8,128)S(1)}, f32[256,1024]{1,0:T(8,128)}, u32[]{:S(2)}, u32[]{:S(2)}) collective-permute-start(f32[256,1024]{1,0:T(8,128)S(1)} %fusion.5), channel_id=1, source_target_pairs={{0,8},{1,9},{2,10},{3,11},{4,12},{5,13},{6,14},{7,15},{8,0},{9,1},... | collective-permute-start | bytes 3145736 | tf_op jit(solution)/shard_map/ppermute | solution.py:8
  95.5 0.6 iota_compare_fusion.3
  96.1 2.0 fusion.22
  98.1 43.2 %collective-permute-done.3 = f32[256,1024]{1,0:T(8,128)} collective-permute-done((f32[256,1024]{1,0:T(8,128)S(1)}, f32[256,1024]{1,0:T(8,128)}, u32[]{:S(2)}, u32[]{:S(2)}) %collective-permute-start.3) | collective-permute-done | bytes 1048608 | tf_op jit(solution)/shard_map/ppermute | solution.py:8
  141.3 2.4 fusion.4
  143.7 3.3 %collective-permute-start.4 = (f32[256,1024]{1,0:T(8,128)S(1)}, f32[256,1024]{1,0:T(8,128)}, u32[]{:S(2)}, u32[]{:S(2)}) collective-permute-start(f32[256,1024]{1,0:T(8,128)S(1)} %fusion.4), channel_id=1, source_target_pairs={{0,16},{1,17},{2,18},{3,19},{4,20},{5,21},{6,22},{7,23},{8,24},{9,... | collective-permute-start | bytes 3145736 | tf_op jit(solution)/shard_map/ppermute | solution.py:8
  147.0 0.6 iota_compare_fusion.4
  147.6 1.0 fusion.24
  148.7 20.8 %collective-permute-done.4 = f32[256,1024]{1,0:T(8,128)} collective-permute-done((f32[256,1024]{1,0:T(8,128)S(1)}, f32[256,1024]{1,0:T(8,128)}, u32[]{:S(2)}, u32[]{:S(2)}) %collective-permute-start.4) | collective-permute-done | bytes 1048608 | tf_op jit(solution)/shard_map/ppermute | solution.py:8
  169.5 2.3 fusion.3
  171.8 1.6 collective-permute-start.5
  173.3 0.6 iota_compare_fusion.5
  173.9 1.0 fusion.26
  174.9 20.0 %collective-permute-done.5 = f32[256,1024]{1,0:T(8,128)} collective-permute-done((f32[256,1024]{1,0:T(8,128)S(1)}, f32[256,1024]{1,0:T(8,128)}, u32[]{:S(2)}, u32[]{:S(2)}) %collective-permute-start.5) | collective-permute-done | bytes 1048608 | tf_op jit(solution)/shard_map/ppermute | solution.py:8
  195.0 2.3 fusion.2
  197.2 0.6 collective-permute-start.6
  197.9 0.7 iota_compare_fusion.6
  198.6 1.0 fusion.28
  199.6 19.9 %collective-permute-done.6 = f32[256,1024]{1,0:T(8,128)} collective-permute-done((f32[256,1024]{1,0:T(8,128)S(1)}, f32[256,1024]{1,0:T(8,128)}, u32[]{:S(2)}, u32[]{:S(2)}) %collective-permute-start.6) | collective-permute-done | bytes 1048608 | tf_op jit(solution)/shard_map/ppermute | solution.py:8
  219.5 2.3 fusion.1
  221.8 2.4 collective-permute-start.7
  224.2 0.7 iota_compare_fusion.7
  224.9 1.0 fusion.30
  225.9 18.7 %collective-permute-done.7 = f32[256,1024]{1,0:T(8,128)} collective-permute-done((f32[256,1024]{1,0:T(8,128)S(1)}, f32[256,1024]{1,0:T(8,128)}, u32[]{:S(2)}, u32[]{:S(2)}) %collective-permute-start.7) | collective-permute-done | bytes 1048608 | tf_op jit(solution)/shard_map/ppermute | solution.py:8
  244.7 3.2 %fusion = f32[256,1024]{1,0:T(8,128)} fusion(f32[256,1024]{1,0:T(8,128)S(1)} %fusion.30, f32[256,1024]{1,0:T(8,128)} %collective-permute-done.7, pred[256]{0:T(512)(128)(4,1)S(1)} %iota_compare_fusion.7, f32[1,256,512]{2,1,0:T(8,128)S(1)} %get-tuple-element.5, s32[]{:T(128)S(6)} %select_n.95), kind=kOutput, calls=%fused_computation.1 | convolution fusion | flops 805830656 | bytes 3408388 | tf_op jit(solution)/shard_map/dot_general | solution.py:19
Async XLA Ops:
  0.0 7.1 %collective-permute-start = (f32[256,1024]{1,0:T(8,128)}, f32[256,1024]{1,0:T(8,128)}, u32[]{:S(2)}, u32[]{:S(2)}) collective-permute-start(f32[256,1024]{1,0:T(8,128)} %param.3), channel_id=1, source_target_pairs={{0,1},{1,0},{2,3},{3,2},{4,5},{5,4},{6,7},{7,6},{8,9},{9,8},{10,11... | collective-permute-start | bytes 3145736 | tf_op jit(solution)/shard_map/ppermute | solution.py:8
  2.3 3.8 %copy-start = (f32[256,1024]{1,0:T(8,128)S(1)}, f32[256,1024]{1,0:T(8,128)}, u32[]{:S(2)}) copy-start(f32[256,1024]{1,0:T(8,128)} %param.3) | copy-start | bytes 3145732
  9.4 25.9 %collective-permute-start.1 = (f32[256,1024]{1,0:T(8,128)S(1)}, f32[256,1024]{1,0:T(8,128)}, u32[]{:S(2)}, u32[]{:S(2)}) collective-permute-start(f32[256,1024]{1,0:T(8,128)S(1)} %fusion.7), channel_id=1, source_target_pairs={{0,2},{1,3},{2,0},{3,1},{4,6},{5,7},{6,4},{7,5},{8,10},{9,11},{10,... | collective-permute-start | bytes 3145736 | tf_op jit(solution)/shard_map/ppermute | solution.py:8
  37.7 49.1 %collective-permute-start.2 = (f32[256,1024]{1,0:T(8,128)S(1)}, f32[256,1024]{1,0:T(8,128)}, u32[]{:S(2)}, u32[]{:S(2)}) collective-permute-start(f32[256,1024]{1,0:T(8,128)S(1)} %fusion.6), channel_id=1, source_target_pairs={{0,4},{1,5},{2,6},{3,7},{4,0},{5,1},{6,2},{7,3},{8,12},{9,13},{10,... | collective-permute-start | bytes 3145736 | tf_op jit(solution)/shard_map/ppermute | solution.py:8
  89.2 52.1 %collective-permute-start.3 = (f32[256,1024]{1,0:T(8,128)S(1)}, f32[256,1024]{1,0:T(8,128)}, u32[]{:S(2)}, u32[]{:S(2)}) collective-permute-start(f32[256,1024]{1,0:T(8,128)S(1)} %fusion.5), channel_id=1, source_target_pairs={{0,8},{1,9},{2,10},{3,11},{4,12},{5,13},{6,14},{7,15},{8,0},{9,1},... | collective-permute-start | bytes 3145736 | tf_op jit(solution)/shard_map/ppermute | solution.py:8
  143.7 25.8 %collective-permute-start.4 = (f32[256,1024]{1,0:T(8,128)S(1)}, f32[256,1024]{1,0:T(8,128)}, u32[]{:S(2)}, u32[]{:S(2)}) collective-permute-start(f32[256,1024]{1,0:T(8,128)S(1)} %fusion.4), channel_id=1, source_target_pairs={{0,16},{1,17},{2,18},{3,19},{4,20},{5,21},{6,22},{7,23},{8,24},{9,... | collective-permute-start | bytes 3145736 | tf_op jit(solution)/shard_map/ppermute | solution.py:8
  171.8 23.2 %collective-permute-start.5 = (f32[256,1024]{1,0:T(8,128)S(1)}, f32[256,1024]{1,0:T(8,128)}, u32[]{:S(2)}, u32[]{:S(2)}) collective-permute-start(f32[256,1024]{1,0:T(8,128)S(1)} %fusion.3), channel_id=1, source_target_pairs={{0,32},{32,0},{64,96},{96,64},{128,160},{160,128},{192,224},{224,1... | collective-permute-start | bytes 3145736 | tf_op jit(solution)/shard_map/ppermute | solution.py:8
  197.2 22.3 %collective-permute-start.6 = (f32[256,1024]{1,0:T(8,128)S(1)}, f32[256,1024]{1,0:T(8,128)}, u32[]{:S(2)}, u32[]{:S(2)}) collective-permute-start(f32[256,1024]{1,0:T(8,128)S(1)} %fusion.2), channel_id=1, source_target_pairs={{0,64},{32,96},{64,0},{96,32},{128,192},{160,224},{192,128},{224,1... | collective-permute-start | bytes 3145736 | tf_op jit(solution)/shard_map/ppermute | solution.py:8
  221.8 22.9 %collective-permute-start.7 = (f32[256,1024]{1,0:T(8,128)S(1)}, f32[256,1024]{1,0:T(8,128)}, u32[]{:S(2)}, u32[]{:S(2)}) collective-permute-start(f32[256,1024]{1,0:T(8,128)S(1)} %fusion.1), channel_id=1, source_target_pairs={{0,128},{32,160},{64,192},{96,224},{128,0},{160,32},{192,64},{224,... | collective-permute-start | bytes 3145736 | tf_op jit(solution)/shard_map/ppermute | solution.py:8
where the time goes:
time: 249 us; the launch traced here: 248 us
  waiting for transfers between devices  187 us (75%)
  matrix products  30.5 us (12%)
  starting transfers between devices  19.7 us (8%)
  local copies, waits for them, and re-layouts  5.39 us (2%)
  other arithmetic  4.99 us (2%)
    ppermute x8, waiting for transfers between devices, from_partner(): lax.ppermute(x, axis, [(i, i ^ 1 << stride) for i in range(lax.axis_size(...  187 us
    ppermute x8, starting transfers between devices, from_partner(): lax.ppermute(x, axis, [(i, i ^ 1 << stride) for i in range(lax.axis_size(...  19.7 us
    dot_general x8, matrix products, apply_level(): jnp.dot(other_cols, partner, precision=lax.Precision.HIGHEST, preferred_e...  19.4 us
    dot_general x8, matrix products, apply_level(): jnp.dot(own_cols, current, precision=lax.Precision.HIGHEST, preferred_ele...  11.1 us
    lt x8, other arithmetic, apply_level(): return jnp.where((row_ids < limit)[:, None], mixed, jnp.zeros_like(mixed))  4.99 us
  transfers between devices with their start and end apart: 8, of which 7 were waited for; matrix products, arithmetic and copies ran while one was open for 9% of the time, Pallas kernels for 0%

commit v1 on v0

v1 whole, which is shorter than its diff:
```python
import jax
import jax.numpy as jnp
from jax import lax
from jax.sharding import PartitionSpec as P

WIDTHS = (256, 256, 256, 256)
ORDER = ((0, 0), (0, 1), (1, 0), (0, 2), (1, 1), (2, 0), (0, 3), (1, 2), (2, 1), (3, 0), (0, 4), (1, 3), (2, 2), (3, 1), (0, 5), (1, 4), (2, 3), (3, 2), (0, 6), (1, 5), (2, 4), (3, 3), (0, 7), (1, 6), (2, 5), (3, 4), (1, 7), (2, 6), (3, 5), (2, 7), (3, 6), (3, 7))


def per_device(coefficients, transfer, ranks):
    node_bits = lax.axis_size("node").bit_length() - 1
    group_bits = lax.axis_size("grp").bit_length() - 1
    levels = node_bits + group_bits
    width = coefficients.shape[0]
    node_place, group_place = lax.axis_index("node"), lax.axis_index("grp")
    starts = [sum(WIDTHS[:i]) for i in range(len(WIDTHS))]

    def place(level):
        if level < node_bits:
            return "node", level, node_place >> level & 1
        return "grp", level - node_bits, group_place >> (level - node_bits) & 1

    def exchange(values, level):
        axis, bit, _ = place(level)
        return lax.ppermute(values, axis, [(i, i ^ 1 << bit) for i in range(lax.axis_size(axis))])

    def halves(matrices, limits, level):
        upper = place(level)[2]
        rows = lax.broadcasted_iota(jnp.int32, matrices.shape[1:], 0)
        matrix = jnp.where(rows < limits[level, 0], matrices[level], 0.0)
        return (
            lax.dynamic_slice_in_dim(matrix, upper * width, width, 1),
            lax.dynamic_slice_in_dim(matrix, (1 - upper) * width, width, 1),
        )

    def dot(a, b):
        return jnp.dot(a, b, precision=lax.Precision.HIGH, preferred_element_type=jnp.float32)

    def columns(values, chunk):
        return values[:, starts[chunk] : starts[chunk] + WIDTHS[chunk]]

    from_core = exchange(coefficients, 0)
    own, other = halves(transfer, ranks, 0)
    halved = {0: (own, other)}
    state, partner = {}, {}
    last = None
    for chunk, level in ORDER:
        if level == 0:
            mine, got = columns(coefficients, chunk), columns(from_core, chunk)
        else:
            mine, got = state[chunk], partner[chunk]
        if last is not None:
            mine, last = lax.optimization_barrier((mine, last))
        if level not in halved:
            halved[level] = halves(transfer, ranks, level)
        own, other = halved[level]
        first = dot(own, mine)
        if level:
            got, first = lax.optimization_barrier((got, first))
        state[chunk] = last = first + dot(other, got)
        if (chunk, level) == ORDER[0]:
            transfer, ranks, last = lax.optimization_barrier((transfer, ranks, last))
        if level + 1 < levels:
            partner[chunk] = exchange(state[chunk], level + 1)
    return jnp.concatenate([state[chunk] for chunk in range(len(WIDTHS))], axis=1)


def solution(mesh):
    return jax.shard_map(
        per_device,
        mesh=mesh,
        in_specs=(
            P(("grp", "node"), None),
            P(None, ("grp", "node"), None),
            P(None, ("grp", "node")),
        ),
        out_specs=P(("grp", "node"), None),
        check_vma=False,
    )
```

time: 249 us -> 176 us (0.71)
  waiting for transfers between devices: 187 us -> 87.3 us
  starting transfers between devices: 19.7 us -> 58.2 us
  matrix products: 30.5 us -> 18.4 us
  other arithmetic: 4.99 us -> 9.4 us
  local copies, waits for them, and re-layouts: 5.39 us -> 1.84 us
    ppermute x8 -> x29, waiting for transfers between devices: 187 us -> 87.3 us  [exchange(): lax.ppermute(values, axis, [(i, i ^ 1 << bit) for i in range(lax.axis_siz...]
    ppermute x8 -> x29, starting transfers between devices: 19.7 us -> 58.2 us  [exchange(): lax.ppermute(values, axis, [(i, i ^ 1 << bit) for i in range(lax.axis_siz...]
    dot_general x16 -> x64, matrix products: 30.5 us -> 18.4 us  [dot(): jnp.dot(a, b, precision=lax.Precision.HIGH, preferred_element_type=jnp.fl...]
    slice x2, local copies, waits for them, and re-layouts: 5.38 us -> 1.83 us  [the longest x1 1.17 us: columns(): return values[:, starts[chunk]:starts[chunk] + WIDTHS[chunk]]]
    lt x8 -> x5, other arithmetic: 4.99 us -> 5.25 us  [halves(): matrix = jnp.where(rows < limits[level, 0], matrices[level], 0.0)]
  transfers between devices with their start and end apart: 8 -> 29, of which waited for: 7 -> 15; matrix products, arithmetic and copies ran while one was open for 9% -> 16% of each run, Pallas kernels for 0% -> 0%
where the time goes in v1:
time: 176 us
  waiting for transfers between devices  87.3 us (50%)
  starting transfers between devices  58.2 us (33%)
  matrix products  18.4 us (10%)
  other arithmetic  9.4 us (5%)
  local copies, waits for them, and re-layouts  1.84 us (1%)
    ppermute x29, waiting for transfers between devices, exchange(): lax.ppermute(values, axis, [(i, i ^ 1 << bit) for i in range(lax.axis_siz...  87.3 us
    ppermute x29, starting transfers between devices, exchange(): lax.ppermute(values, axis, [(i, i ^ 1 << bit) for i in range(lax.axis_siz...  58.2 us
    dot_general x64, matrix products, dot(): jnp.dot(a, b, precision=lax.Precision.HIGH, preferred_element_type=jnp.fl...  18.4 us
    lt x5, other arithmetic, halves(): matrix = jnp.where(rows < limits[level, 0], matrices[level], 0.0)  5.25 us
  transfers between devices with their start and end apart: 29, of which 15 were waited for; matrix products, arithmetic and copies ran while one was open for 16% of the time, Pallas kernels for 0%

profile of v1, /device:TPU:8, one launch (start us, length us, event | category | flops | bytes accessed | tf_op | source)
XLA Modules:
  0.0 176.1 jit_solution(10896020556104156164)
XLA Ops:
  0.0 0.8 iota_compare_fusion.7
  0.8 1.6 bitcast_select_fusion.7
  2.4 1.2 fusion.4
  3.6 1.2 fusion.193
  4.8 0.3 convolution_add_fusion.3
  5.1 2.0 %collective-permute-start.1 = (f32[256,256]{1,0:T(8,128)S(1)}, f32[256,256]{1,0:T(8,128)S(1)}, u32[]{:S(2)}, u32[]{:S(2)}) collective-permute-start(f32[256,256]{1,0:T(8,128)S(1)} %convolution_add_fusion.3), channel_id=1, source_target_pairs={{0,2},{1,3},{2,0},{3,1},{4,6},{5,7},{6,4},{7,5},{8,10},{9,11},{10,... | collective-permute-start | bytes 786440 | tf_op jit(solution)/shard_map/ppermute | solution.py:25
  7.1 0.7 fusion.194
  7.8 0.6 iota_compare_fusion.6
  8.4 1.2 iota_compare_fusion.4
  9.7 1.2 iota_compare_fusion.2
  10.9 1.3 iota_compare_fusion
  12.3 0.5 bitcast_select_fusion
  12.8 0.3 fusion.116
  13.0 0.8 collective-permute-done.1
  14.1 3.4 %collective-permute-start.2 = (f32[256,256]{1,0:T(8,128)S(1)}, f32[256,256]{1,0:T(8,128)S(1)}, u32[]{:S(2)}, u32[]{:S(2)}) collective-permute-start(f32[256,256]{1,0:T(8,128)S(1)} %add.149), channel_id=1, source_target_pairs={{0,4},{1,5},{2,6},{3,7},{4,0},{5,1},{6,2},{7,3},{8,12},{9,13},{10,... | collective-permute-start | bytes 786440 | tf_op jit(solution)/shard_map/ppermute | solution.py:25
  17.8 0.3 convolution_add_fusion.2
  18.1 1.8 %collective-permute-start.4 = (f32[256,256]{1,0:T(8,128)S(1)}, f32[256,256]{1,0:T(8,128)S(1)}, u32[]{:S(2)}, u32[]{:S(2)}) collective-permute-start(f32[256,256]{1,0:T(8,128)S(1)} %convolution_add_fusion.2), channel_id=1, source_target_pairs={{0,2},{1,3},{2,0},{3,1},{4,6},{5,7},{6,4},{7,5},{8,10},{9,11},{10,... | collective-permute-start | bytes 786440 | tf_op jit(solution)/shard_map/ppermute | solution.py:25
  20.2 9.2 %collective-permute-done.2 = f32[256,256]{1,0:T(8,128)S(1)} collective-permute-done((f32[256,256]{1,0:T(8,128)S(1)}, f32[256,256]{1,0:T(8,128)S(1)}, u32[]{:S(2)}, u32[]{:S(2)}) %collective-permute-start.2) | collective-permute-done | bytes 262176 | tf_op jit(solution)/shard_map/ppermute | solution.py:25
  29.6 6.3 %collective-permute-start.3 = (f32[256,256]{1,0:T(8,128)S(1)}, f32[256,256]{1,0:T(8,128)S(1)}, u32[]{:S(2)}, u32[]{:S(2)}) collective-permute-start(f32[256,256]{1,0:T(8,128)S(1)} %add.153), channel_id=1, source_target_pairs={{0,8},{1,9},{2,10},{3,11},{4,12},{5,13},{6,14},{7,15},{8,0},{9,1},... | collective-permute-start | bytes 786440 | tf_op jit(solution)/shard_map/ppermute | solution.py:25
  36.2 0.3 fusion.106
  36.9 0.3 convolution_add_fusion.1
  37.2 2.5 %collective-permute-start.6 = (f32[256,256]{1,0:T(8,128)S(1)}, f32[256,256]{1,0:T(8,128)S(1)}, u32[]{:S(2)}, u32[]{:S(2)}) collective-permute-start(f32[256,256]{1,0:T(8,128)S(1)} %convolution_add_fusion.1), channel_id=1, source_target_pairs={{0,2},{1,3},{2,0},{3,1},{4,6},{5,7},{6,4},{7,5},{8,10},{9,11},{10,... | collective-permute-start | bytes 786440 | tf_op jit(solution)/shard_map/ppermute | solution.py:25
  40.0 8.1 %collective-permute-done.3 = f32[256,256]{1,0:T(8,128)S(1)} collective-permute-done((f32[256,256]{1,0:T(8,128)S(1)}, f32[256,256]{1,0:T(8,128)S(1)}, u32[]{:S(2)}, u32[]{:S(2)}) %collective-permute-start.3) | collective-permute-done | bytes 262176 | tf_op jit(solution)/shard_map/ppermute | solution.py:25
  48.4 3.1 %collective-permute-start.5 = (f32[256,256]{1,0:T(8,128)S(1)}, f32[256,256]{1,0:T(8,128)S(1)}, u32[]{:S(2)}, u32[]{:S(2)}) collective-permute-start(f32[256,256]{1,0:T(8,128)S(1)} %add.158), channel_id=1, source_target_pairs={{0,16},{1,17},{2,18},{3,19},{4,20},{5,21},{6,22},{7,23},{8,24},{9,... | collective-permute-start | bytes 786440 | tf_op jit(solution)/shard_map/ppermute | solution.py:25
  51.8 6.9 %collective-permute-done.7 = f32[256,256]{1,0:T(8,128)S(1)} collective-permute-done((f32[256,256]{1,0:T(8,128)S(1)}, f32[256,256]{1,0:T(8,128)S(1)}, u32[]{:S(2)}, u32[]{:S(2)}) %collective-permute-start.7) | collective-permute-done | bytes 262176 | tf_op jit(solution)/shard_map/ppermute | solution.py:25
  59.1 3.4 %collective-permute-start.11 = (f32[256,256]{1,0:T(8,128)S(1)}, f32[256,256]{1,0:T(8,128)S(1)}, u32[]{:S(2)}, u32[]{:S(2)}) collective-permute-start(f32[256,256]{1,0:T(8,128)S(1)} %add.160), channel_id=1, source_target_pairs={{0,8},{1,9},{2,10},{3,11},{4,12},{5,13},{6,14},{7,15},{8,0},{9,1},... | collective-permute-start | bytes 786440 | tf_op jit(solution)/shard_map/ppermute | solution.py:25
  63.2 0.3 fusion.122
  63.5 0.3 convolution_add_fusion
  63.8 1.1 collective-permute-start.9
  65.2 0.3 fusion.60
  65.5 1.8 %collective-permute-start.8 = (f32[256,256]{1,0:T(8,128)S(1)}, f32[256,256]{1,0:T(8,128)S(1)}, u32[]{:S(2)}, u32[]{:S(2)}) collective-permute-start(f32[256,256]{1,0:T(8,128)S(1)} %add.164), channel_id=1, source_target_pairs={{0,32},{32,0},{64,96},{96,64},{128,160},{160,128},{192,224},{224,1... | collective-permute-start | bytes 786440 | tf_op jit(solution)/shard_map/ppermute | solution.py:25
  67.6 9.4 %collective-permute-done.11 = f32[256,256]{1,0:T(8,128)S(1)} collective-permute-done((f32[256,256]{1,0:T(8,128)S(1)}, f32[256,256]{1,0:T(8,128)S(1)}, u32[]{:S(2)}, u32[]{:S(2)}) %collective-permute-start.11) | collective-permute-done | bytes 262176 | tf_op jit(solution)/shard_map/ppermute | solution.py:25
  77.3 3.1 %collective-permute-start.15 = (f32[256,256]{1,0:T(8,128)S(1)}, f32[256,256]{1,0:T(8,128)S(1)}, u32[]{:S(2)}, u32[]{:S(2)}) collective-permute-start(f32[256,256]{1,0:T(8,128)S(1)} %add.166), channel_id=1, source_target_pairs={{0,16},{1,17},{2,18},{3,19},{4,20},{5,21},{6,22},{7,23},{8,24},{9,... | collective-permute-start | bytes 786440 | tf_op jit(solution)/shard_map/ppermute | solution.py:25
  80.7 5.2 %collective-permute-done.10 = f32[256,256]{1,0:T(8,128)S(1)} collective-permute-done((f32[256,256]{1,0:T(8,128)S(1)}, f32[256,256]{1,0:T(8,128)S(1)}, u32[]{:S(2)}, u32[]{:S(2)}) %collective-permute-start.10) | collective-permute-done | bytes 262176 | tf_op jit(solution)/shard_map/ppermute | solution.py:25
  86.2 2.8 %collective-permute-start.14 = (f32[256,256]{1,0:T(8,128)S(1)}, f32[256,256]{1,0:T(8,128)S(1)}, u32[]{:S(2)}, u32[]{:S(2)}) collective-permute-start(f32[256,256]{1,0:T(8,128)S(1)} %add.167), channel_id=1, source_target_pairs={{0,8},{1,9},{2,10},{3,11},{4,12},{5,13},{6,14},{7,15},{8,0},{9,1},... | collective-permute-start | bytes 786440 | tf_op jit(solution)/shard_map/ppermute | solution.py:25
  89.3 0.3 fusion.102
  90.3 1.0 collective-permute-start.12
  91.6 0.3 fusion.58
  91.9 1.1 collective-permute-start.19
  93.4 10.2 %collective-permute-done.14 = f32[256,256]{1,0:T(8,128)S(1)} collective-permute-done((f32[256,256]{1,0:T(8,128)S(1)}, f32[256,256]{1,0:T(8,128)S(1)}, u32[]{:S(2)}, u32[]{:S(2)}) %collective-permute-start.14) | collective-permute-done | bytes 262176 | tf_op jit(solution)/shard_map/ppermute | solution.py:25
  103.9 3.1 %collective-permute-start.18 = (f32[256,256]{1,0:T(8,128)S(1)}, f32[256,256]{1,0:T(8,128)S(1)}, u32[]{:S(2)}, u32[]{:S(2)}) collective-permute-start(f32[256,256]{1,0:T(8,128)S(1)} %add.173), channel_id=1, source_target_pairs={{0,16},{1,17},{2,18},{3,19},{4,20},{5,21},{6,22},{7,23},{8,24},{9,... | collective-permute-start | bytes 786440 | tf_op jit(solution)/shard_map/ppermute | solution.py:25
  107.3 7.3 %collective-permute-done.13 = f32[256,256]{1,0:T(8,128)S(1)} collective-permute-done((f32[256,256]{1,0:T(8,128)S(1)}, f32[256,256]{1,0:T(8,128)S(1)}, u32[]{:S(2)}, u32[]{:S(2)}) %collective-permute-start.13) | collective-permute-done | bytes 262176 | tf_op jit(solution)/shard_map/ppermute | solution.py:25
  115.0 3.3 %collective-permute-start.17 = (f32[256,256]{1,0:T(8,128)S(1)}, f32[256,256]{1,0:T(8,128)S(1)}, u32[]{:S(2)}, u32[]{:S(2)}) collective-permute-start(f32[256,256]{1,0:T(8,128)S(1)} %add.174), channel_id=1, source_target_pairs={{0,8},{1,9},{2,10},{3,11},{4,12},{5,13},{6,14},{7,15},{8,0},{9,1},... | collective-permute-start | bytes 786440 | tf_op jit(solution)/shard_map/ppermute | solution.py:25
  118.9 2.4 %collective-permute-start.16 = (f32[256,256]{1,0:T(8,128)S(1)}, f32[256,256]{1,0:T(8,128)S(1)}, u32[]{:S(2)}, u32[]{:S(2)}) collective-permute-start(f32[256,256]{1,0:T(8,128)S(1)} %add.176), channel_id=1, source_target_pairs={{0,128},{32,160},{64,192},{96,224},{128,0},{160,32},{192,64},{224,... | collective-permute-start | bytes 786440 | tf_op jit(solution)/shard_map/ppermute | solution.py:25
  121.5 0.3 fusion.42
  121.9 1.4 collective-permute-start.20
  123.9 1.6 collective-permute-start.23
  125.8 6.8 %collective-permute-done.17 = f32[256,256]{1,0:T(8,128)S(1)} collective-permute-done((f32[256,256]{1,0:T(8,128)S(1)}, f32[256,256]{1,0:T(8,128)S(1)}, u32[]{:S(2)}, u32[]{:S(2)}) %collective-permute-start.17) | collective-permute-done | bytes 262176 | tf_op jit(solution)/shard_map/ppermute | solution.py:25
  132.9 3.3 %collective-permute-start.22 = (f32[256,256]{1,0:T(8,128)S(1)}, f32[256,256]{1,0:T(8,128)S(1)}, u32[]{:S(2)}, u32[]{:S(2)}) collective-permute-start(f32[256,256]{1,0:T(8,128)S(1)} %add.180), channel_id=1, source_target_pairs={{0,16},{1,17},{2,18},{3,19},{4,20},{5,21},{6,22},{7,23},{8,24},{9,... | collective-permute-start | bytes 786440 | tf_op jit(solution)/shard_map/ppermute | solution.py:25
  136.9 0.3 fusion.34
  137.5 2.4 %collective-permute-start.21 = (f32[256,256]{1,0:T(8,128)S(1)}, f32[256,256]{1,0:T(8,128)S(1)}, u32[]{:S(2)}, u32[]{:S(2)}) collective-permute-start(f32[256,256]{1,0:T(8,128)S(1)} %add.183), channel_id=1, source_target_pairs={{0,128},{32,160},{64,192},{96,224},{128,0},{160,32},{192,64},{224,... | collective-permute-start | bytes 786440 | tf_op jit(solution)/shard_map/ppermute | solution.py:25
  140.5 1.4 collective-permute-start.24
  142.2 0.7 collective-permute-done.22
  143.3 1.6 collective-permute-start.26
  145.2 3.1 %collective-permute-done.21 = f32[256,256]{1,0:T(8,128)S(1)} collective-permute-done((f32[256,256]{1,0:T(8,128)S(1)}, f32[256,256]{1,0:T(8,128)S(1)}, u32[]{:S(2)}, u32[]{:S(2)}) %collective-permute-start.21) | collective-permute-done | bytes 262176 | tf_op jit(solution)/shard_map/ppermute | solution.py:25
  148.9 3.9 %collective-permute-done.24 = f32[256,256]{1,0:T(8,128)S(1)} collective-permute-done((f32[256,256]{1,0:T(8,128)S(1)}, f32[256,256]{1,0:T(8,128)S(1)}, u32[]{:S(2)}, u32[]{:S(2)}) %collective-permute-start.24) | collective-permute-done | bytes 262176 | tf_op jit(solution)/shard_map/ppermute | solution.py:25
  153.2 0.3 fusion.46
  153.8 2.6 %collective-permute-start.27 = (f32[256,256]{1,0:T(8,128)S(1)}, f32[256,256]{1,0:T(8,128)S(1)}, u32[]{:S(2)}, u32[]{:S(2)}) collective-permute-start(f32[256,256]{1,0:T(8,128)S(1)} %add.188), channel_id=1, source_target_pairs={{0,64},{32,96},{64,0},{96,32},{128,192},{160,224},{192,128},{224,1... | collective-permute-start | bytes 786440 | tf_op jit(solution)/shard_map/ppermute | solution.py:25
  156.7 7.3 %collective-permute-done.25 = f32[256,256]{1,0:T(8,128)S(1)} collective-permute-done((f32[256,256]{1,0:T(8,128)S(1)}, f32[256,256]{1,0:T(8,128)S(1)}, u32[]{:S(2)}, u32[]{:S(2)}) %collective-permute-start.25) | collective-permute-done | bytes 262176 | tf_op jit(solution)/shard_map/ppermute | solution.py:25
  164.3 0.3 fusion.30
  164.6 1.8 %collective-permute-done.27 = f32[256,256]{1,0:T(8,128)S(1)} collective-permute-done((f32[256,256]{1,0:T(8,128)S(1)}, f32[256,256]{1,0:T(8,128)S(1)}, u32[]{:S(2)}, u32[]{:S(2)}) %collective-permute-start.27) | collective-permute-done | bytes 262176 | tf_op jit(solution)/shard_map/ppermute | solution.py:25
  166.7 1.2 collective-permute-start.28
  168.2 6.5 %collective-permute-done.28 = f32[256,256]{1,0:T(8,128)S(1)} collective-permute-done((f32[256,256]{1,0:T(8,128)S(1)}, f32[256,256]{1,0:T(8,128)S(1)}, u32[]{:S(2)}, u32[]{:S(2)}) %collective-permute-start.28) | collective-permute-done | bytes 262176 | tf_op jit(solution)/shard_map/ppermute | solution.py:25
  175.0 1.1 pad_maximum_fusion
  (100 shorter events, 14.7 us)
Async XLA Ops:
  0.0 7.1 %copy-start.1 = (s32[8,1]{0,1:T(1,128)S(1)}, s32[8,1]{0,1:T(1,128)}, u32[]{:S(2)}) copy-start(s32[8,1]{0,1:T(1,128)} %param.5) | copy-start | bytes 100
  0.0 4.8 %collective-permute-start = (f32[256,1024]{1,0:T(8,128)}, f32[256,1024]{1,0:T(8,128)S(1)}, u32[]{:S(2)}, u32[]{:S(2)}) collective-permute-start(f32[256,1024]{1,0:T(8,128)} %param.3), channel_id=1, source_target_pairs={{0,1},{1,0},{2,3},{3,2},{4,5},{5,4},{6,7},{7,6},{8,9},{9,8},{10,11... | collective-permute-start | bytes 3145736 | tf_op jit(solution)/shard_map/ppermute | solution.py:25
  0.0 12.3 %copy-start = (f32[8,256,512]{2,1,0:T(8,128)S(1)}, f32[8,256,512]{2,1,0:T(8,128)}, u32[]{:S(2)}) copy-start(f32[8,256,512]{2,1,0:T(8,128)} %param.4) | copy-start | bytes 12582916
  5.1 8.7 %collective-permute-start.1 = (f32[256,256]{1,0:T(8,128)S(1)}, f32[256,256]{1,0:T(8,128)S(1)}, u32[]{:S(2)}, u32[]{:S(2)}) collective-permute-start(f32[256,256]{1,0:T(8,128)S(1)} %convolution_add_fusion.3), channel_id=1, source_target_pairs={{0,2},{1,3},{2,0},{3,1},{4,6},{5,7},{6,4},{7,5},{8,10},{9,11},{10,... | collective-permute-start | bytes 786440 | tf_op jit(solution)/shard_map/ppermute | solution.py:25
  14.1 15.2 %collective-permute-start.2 = (f32[256,256]{1,0:T(8,128)S(1)}, f32[256,256]{1,0:T(8,128)S(1)}, u32[]{:S(2)}, u32[]{:S(2)}) collective-permute-start(f32[256,256]{1,0:T(8,128)S(1)} %add.149), channel_id=1, source_target_pairs={{0,4},{1,5},{2,6},{3,7},{4,0},{5,1},{6,2},{7,3},{8,12},{9,13},{10,... | collective-permute-start | bytes 786440 | tf_op jit(solution)/shard_map/ppermute | solution.py:25
  18.1 18.1 %collective-permute-start.4 = (f32[256,256]{1,0:T(8,128)S(1)}, f32[256,256]{1,0:T(8,128)S(1)}, u32[]{:S(2)}, u32[]{:S(2)}) collective-permute-start(f32[256,256]{1,0:T(8,128)S(1)} %convolution_add_fusion.2), channel_id=1, source_target_pairs={{0,2},{1,3},{2,0},{3,1},{4,6},{5,7},{6,4},{7,5},{8,10},{9,11},{10,... | collective-permute-start | bytes 786440 | tf_op jit(solution)/shard_map/ppermute | solution.py:25
  29.6 18.5 %collective-permute-start.3 = (f32[256,256]{1,0:T(8,128)S(1)}, f32[256,256]{1,0:T(8,128)S(1)}, u32[]{:S(2)}, u32[]{:S(2)}) collective-permute-start(f32[256,256]{1,0:T(8,128)S(1)} %add.153), channel_id=1, source_target_pairs={{0,8},{1,9},{2,10},{3,11},{4,12},{5,13},{6,14},{7,15},{8,0},{9,1},... | collective-permute-start | bytes 786440 | tf_op jit(solution)/shard_map/ppermute | solution.py:25
  36.5 22.2 %collective-permute-start.7 = (f32[256,256]{1,0:T(8,128)S(1)}, f32[256,256]{1,0:T(8,128)S(1)}, u32[]{:S(2)}, u32[]{:S(2)}) collective-permute-start(f32[256,256]{1,0:T(8,128)S(1)} %add.155), channel_id=1, source_target_pairs={{0,4},{1,5},{2,6},{3,7},{4,0},{5,1},{6,2},{7,3},{8,12},{9,13},{10,... | collective-permute-start | bytes 786440 | tf_op jit(solution)/shard_map/ppermute | solution.py:25
  37.2 25.6 %collective-permute-start.6 = (f32[256,256]{1,0:T(8,128)S(1)}, f32[256,256]{1,0:T(8,128)S(1)}, u32[]{:S(2)}, u32[]{:S(2)}) collective-permute-start(f32[256,256]{1,0:T(8,128)S(1)} %convolution_add_fusion.1), channel_id=1, source_target_pairs={{0,2},{1,3},{2,0},{3,1},{4,6},{5,7},{6,4},{7,5},{8,10},{9,11},{10,... | collective-permute-start | bytes 786440 | tf_op jit(solution)/shard_map/ppermute | solution.py:25
  48.4 16.7 %collective-permute-start.5 = (f32[256,256]{1,0:T(8,128)S(1)}, f32[256,256]{1,0:T(8,128)S(1)}, u32[]{:S(2)}, u32[]{:S(2)}) collective-permute-start(f32[256,256]{1,0:T(8,128)S(1)} %add.158), channel_id=1, source_target_pairs={{0,16},{1,17},{2,18},{3,19},{4,20},{5,21},{6,22},{7,23},{8,24},{9,... | collective-permute-start | bytes 786440 | tf_op jit(solution)/shard_map/ppermute | solution.py:25
  59.1 17.9 %collective-permute-start.11 = (f32[256,256]{1,0:T(8,128)S(1)}, f32[256,256]{1,0:T(8,128)S(1)}, u32[]{:S(2)}, u32[]{:S(2)}) collective-permute-start(f32[256,256]{1,0:T(8,128)S(1)} %add.160), channel_id=1, source_target_pairs={{0,8},{1,9},{2,10},{3,11},{4,12},{5,13},{6,14},{7,15},{8,0},{9,1},... | collective-permute-start | bytes 786440 | tf_op jit(solution)/shard_map/ppermute | solution.py:25
  63.1 22.7 %collective-permute-start.10 = (f32[256,256]{1,0:T(8,128)S(1)}, f32[256,256]{1,0:T(8,128)S(1)}, u32[]{:S(2)}, u32[]{:S(2)}) collective-permute-start(f32[256,256]{1,0:T(8,128)S(1)} %add.161), channel_id=1, source_target_pairs={{0,4},{1,5},{2,6},{3,7},{4,0},{5,1},{6,2},{7,3},{8,12},{9,13},{10,... | collective-permute-start | bytes 786440 | tf_op jit(solution)/shard_map/ppermute | solution.py:25
  63.8 25.5 %collective-permute-start.9 = (f32[256,256]{1,0:T(8,128)S(1)}, f32[256,256]{1,0:T(8,128)S(1)}, u32[]{:S(2)}, u32[]{:S(2)}) collective-permute-start(f32[256,256]{1,0:T(8,128)S(1)} %convolution_add_fusion), channel_id=1, source_target_pairs={{0,2},{1,3},{2,0},{3,1},{4,6},{5,7},{6,4},{7,5},{8,10},{9,11},{10,... | collective-permute-start | bytes 786440 | tf_op jit(solution)/shard_map/ppermute | solution.py:25
  65.5 24.5 %collective-permute-start.8 = (f32[256,256]{1,0:T(8,128)S(1)}, f32[256,256]{1,0:T(8,128)S(1)}, u32[]{:S(2)}, u32[]{:S(2)}) collective-permute-start(f32[256,256]{1,0:T(8,128)S(1)} %add.164), channel_id=1, source_target_pairs={{0,32},{32,0},{64,96},{96,64},{128,160},{160,128},{192,224},{224,1... | collective-permute-start | bytes 786440 | tf_op jit(solution)/shard_map/ppermute | solution.py:25
  77.3 14.3 %collective-permute-start.15 = (f32[256,256]{1,0:T(8,128)S(1)}, f32[256,256]{1,0:T(8,128)S(1)}, u32[]{:S(2)}, u32[]{:S(2)}) collective-permute-start(f32[256,256]{1,0:T(8,128)S(1)} %add.166), channel_id=1, source_target_pairs={{0,16},{1,17},{2,18},{3,19},{4,20},{5,21},{6,22},{7,23},{8,24},{9,... | collective-permute-start | bytes 786440 | tf_op jit(solution)/shard_map/ppermute | solution.py:25
  86.2 17.4 %collective-permute-start.14 = (f32[256,256]{1,0:T(8,128)S(1)}, f32[256,256]{1,0:T(8,128)S(1)}, u32[]{:S(2)}, u32[]{:S(2)}) collective-permute-start(f32[256,256]{1,0:T(8,128)S(1)} %add.167), channel_id=1, source_target_pairs={{0,8},{1,9},{2,10},{3,11},{4,12},{5,13},{6,14},{7,15},{8,0},{9,1},... | collective-permute-start | bytes 786440 | tf_op jit(solution)/shard_map/ppermute | solution.py:25
  89.6 25.0 %collective-permute-start.13 = (f32[256,256]{1,0:T(8,128)S(1)}, f32[256,256]{1,0:T(8,128)S(1)}, u32[]{:S(2)}, u32[]{:S(2)}) collective-permute-start(f32[256,256]{1,0:T(8,128)S(1)} %add.168), channel_id=1, source_target_pairs={{0,4},{1,5},{2,6},{3,7},{4,0},{5,1},{6,2},{7,3},{8,12},{9,13},{10,... | collective-permute-start | bytes 786440 | tf_op jit(solution)/shard_map/ppermute | solution.py:25
  90.3 28.2 %collective-permute-start.12 = (f32[256,256]{1,0:T(8,128)S(1)}, f32[256,256]{1,0:T(8,128)S(1)}, u32[]{:S(2)}, u32[]{:S(2)}) collective-permute-start(f32[256,256]{1,0:T(8,128)S(1)} %add.170), channel_id=1, source_target_pairs={{0,64},{32,96},{64,0},{96,32},{128,192},{160,224},{192,128},{224,1... | collective-permute-start | bytes 786440 | tf_op jit(solution)/shard_map/ppermute | solution.py:25
  91.9 29.6 %collective-permute-start.19 = (f32[256,256]{1,0:T(8,128)S(1)}, f32[256,256]{1,0:T(8,128)S(1)}, u32[]{:S(2)}, u32[]{:S(2)}) collective-permute-start(f32[256,256]{1,0:T(8,128)S(1)} %add.172), channel_id=1, source_target_pairs={{0,32},{32,0},{64,96},{96,64},{128,160},{160,128},{192,224},{224,1... | collective-permute-start | bytes 786440 | tf_op jit(solution)/shard_map/ppermute | solution.py:25
  103.9 19.7 %collective-permute-start.18 = (f32[256,256]{1,0:T(8,128)S(1)}, f32[256,256]{1,0:T(8,128)S(1)}, u32[]{:S(2)}, u32[]{:S(2)}) collective-permute-start(f32[256,256]{1,0:T(8,128)S(1)} %add.173), channel_id=1, source_target_pairs={{0,16},{1,17},{2,18},{3,19},{4,20},{5,21},{6,22},{7,23},{8,24},{9,... | collective-permute-start | bytes 786440 | tf_op jit(solution)/shard_map/ppermute | solution.py:25
  115.0 17.7 %collective-permute-start.17 = (f32[256,256]{1,0:T(8,128)S(1)}, f32[256,256]{1,0:T(8,128)S(1)}, u32[]{:S(2)}, u32[]{:S(2)}) collective-permute-start(f32[256,256]{1,0:T(8,128)S(1)} %add.174), channel_id=1, source_target_pairs={{0,8},{1,9},{2,10},{3,11},{4,12},{5,13},{6,14},{7,15},{8,0},{9,1},... | collective-permute-start | bytes 786440 | tf_op jit(solution)/shard_map/ppermute | solution.py:25
  118.9 17.7 %collective-permute-start.16 = (f32[256,256]{1,0:T(8,128)S(1)}, f32[256,256]{1,0:T(8,128)S(1)}, u32[]{:S(2)}, u32[]{:S(2)}) collective-permute-start(f32[256,256]{1,0:T(8,128)S(1)} %add.176), channel_id=1, source_target_pairs={{0,128},{32,160},{64,192},{96,224},{128,0},{160,32},{192,64},{224,... | collective-permute-start | bytes 786440 | tf_op jit(solution)/shard_map/ppermute | solution.py:25
  121.9 15.3 %collective-permute-start.20 = (f32[256,256]{1,0:T(8,128)S(1)}, f32[256,256]{1,0:T(8,128)S(1)}, u32[]{:S(2)}, u32[]{:S(2)}) collective-permute-start(f32[256,256]{1,0:T(8,128)S(1)} %add.178), channel_id=1, source_target_pairs={{0,64},{32,96},{64,0},{96,32},{128,192},{160,224},{192,128},{224,1... | collective-permute-start | bytes 786440 | tf_op jit(solution)/shard_map/ppermute | solution.py:25
  123.9 16.3 %collective-permute-start.23 = (f32[256,256]{1,0:T(8,128)S(1)}, f32[256,256]{1,0:T(8,128)S(1)}, u32[]{:S(2)}, u32[]{:S(2)}) collective-permute-start(f32[256,256]{1,0:T(8,128)S(1)} %add.179), channel_id=1, source_target_pairs={{0,32},{32,0},{64,96},{96,64},{128,160},{160,128},{192,224},{224,1... | collective-permute-start | bytes 786440 | tf_op jit(solution)/shard_map/ppermute | solution.py:25
  132.9 10.0 %collective-permute-start.22 = (f32[256,256]{1,0:T(8,128)S(1)}, f32[256,256]{1,0:T(8,128)S(1)}, u32[]{:S(2)}, u32[]{:S(2)}) collective-permute-start(f32[256,256]{1,0:T(8,128)S(1)} %add.180), channel_id=1, source_target_pairs={{0,16},{1,17},{2,18},{3,19},{4,20},{5,21},{6,22},{7,23},{8,24},{9,... | collective-permute-start | bytes 786440 | tf_op jit(solution)/shard_map/ppermute | solution.py:25
  137.5 10.8 %collective-permute-start.21 = (f32[256,256]{1,0:T(8,128)S(1)}, f32[256,256]{1,0:T(8,128)S(1)}, u32[]{:S(2)}, u32[]{:S(2)}) collective-permute-start(f32[256,256]{1,0:T(8,128)S(1)} %add.183), channel_id=1, source_target_pairs={{0,128},{32,160},{64,192},{96,224},{128,0},{160,32},{192,64},{224,... | collective-permute-start | bytes 786440 | tf_op jit(solution)/shard_map/ppermute | solution.py:25
  140.5 12.3 %collective-permute-start.24 = (f32[256,256]{1,0:T(8,128)S(1)}, f32[256,256]{1,0:T(8,128)S(1)}, u32[]{:S(2)}, u32[]{:S(2)}) collective-permute-start(f32[256,256]{1,0:T(8,128)S(1)} %add.184), channel_id=1, source_target_pairs={{0,64},{32,96},{64,0},{96,32},{128,192},{160,224},{192,128},{224,1... | collective-permute-start | bytes 786440 | tf_op jit(solution)/shard_map/ppermute | solution.py:25
  143.3 10.2 %collective-permute-start.26 = (f32[256,256]{1,0:T(8,128)S(1)}, f32[256,256]{1,0:T(8,128)S(1)}, u32[]{:S(2)}, u32[]{:S(2)}) collective-permute-start(f32[256,256]{1,0:T(8,128)S(1)} %add.185), channel_id=1, source_target_pairs={{0,32},{32,0},{64,96},{96,64},{128,160},{160,128},{192,224},{224,1... | collective-permute-start | bytes 786440 | tf_op jit(solution)/shard_map/ppermute | solution.py:25
  153.1 10.8 %collective-permute-start.25 = (f32[256,256]{1,0:T(8,128)S(1)}, f32[256,256]{1,0:T(8,128)S(1)}, u32[]{:S(2)}, u32[]{:S(2)}) collective-permute-start(f32[256,256]{1,0:T(8,128)S(1)} %add.187), channel_id=1, source_target_pairs={{0,128},{32,160},{64,192},{96,224},{128,0},{160,32},{192,64},{224,... | collective-permute-start | bytes 786440 | tf_op jit(solution)/shard_map/ppermute | solution.py:25
  153.8 12.5 %collective-permute-start.27 = (f32[256,256]{1,0:T(8,128)S(1)}, f32[256,256]{1,0:T(8,128)S(1)}, u32[]{:S(2)}, u32[]{:S(2)}) collective-permute-start(f32[256,256]{1,0:T(8,128)S(1)} %add.188), channel_id=1, source_target_pairs={{0,64},{32,96},{64,0},{96,32},{128,192},{160,224},{192,128},{224,1... | collective-permute-start | bytes 786440 | tf_op jit(solution)/shard_map/ppermute | solution.py:25
  166.7 8.0 %collective-permute-start.28 = (f32[256,256]{1,0:T(8,128)S(1)}, f32[256,256]{1,0:T(8,128)S(1)}, u32[]{:S(2)}, u32[]{:S(2)}) collective-permute-start(f32[256,256]{1,0:T(8,128)S(1)} %add.190), channel_id=1, source_target_pairs={{0,128},{32,160},{64,192},{96,224},{128,0},{160,32},{192,64},{224,... | collective-permute-start | bytes 786440 | tf_op jit(solution)/shard_map/ppermute | solution.py:25

commit v2 on v1

v2 whole, which is shorter than its diff:
```python
import functools

import jax
import jax.numpy as jnp
from jax import lax
from jax.experimental import pallas as pl
from jax.experimental.pallas import tpu as pltpu
from jax.sharding import PartitionSpec as P

WIDTHS = (384, 256, 256, 128)
ORDER = ((0, 0), (0, 1), (1, 0), (0, 2), (1, 1), (2, 0), (1, 2), (0, 3), (3, 0), (2, 1), (0, 4), (1, 3), (3, 1), (2, 2), (1, 4), (0, 5), (1, 5), (2, 3), (3, 2), (0, 6), (2, 4), (1, 6), (3, 3), (0, 7), (2, 5), (3, 4), (3, 5), (1, 7), (2, 6), (3, 6), (2, 7), (3, 7))
VMEM = pl.BlockSpec(memory_space=pltpu.VMEM)
SMEM = pl.BlockSpec(memory_space=pltpu.SMEM)
COST = pl.CostEstimate(flops=2000000000, bytes_accessed=4000000, transcendentals=0)


def split(values):
    high = values.astype(jnp.bfloat16)
    return high, (values - high.astype(jnp.float32)).astype(jnp.bfloat16)


def prepare_kernel(first, device_ref, ranks_ref, matrix_ref, out_ref):
    step = pl.program_id(0)
    level = step + first
    width = out_ref.shape[1]
    upper = device_ref[0] >> level & 1
    rows = lax.broadcasted_iota(jnp.int32, (width, width), 0)
    keep = rows < ranks_ref[level, 0]
    for part in range(2):
        start = pl.multiple_of((upper ^ part) * width, width)
        half = jnp.where(keep, matrix_ref[0, :, pl.ds(start, width)], 0.0)
        high, low = split(half)
        for place, term in enumerate((high, high, low)):
            column = (3 * part + place) * width
            out_ref[step, :, column : column + width] = term


def prepare(device, ranks, transfer, first, count):
    _, width, both = transfer.shape
    return pl.pallas_call(
        functools.partial(prepare_kernel, first),
        grid=(count,),
        in_specs=[SMEM, SMEM, pl.BlockSpec((1, width, both), lambda i: (i + first, 0, 0))],
        out_specs=VMEM,
        out_shape=jax.ShapeDtypeStruct((count, width, 3 * both), jnp.bfloat16),
        compiler_params=pltpu.CompilerParams(vmem_limit_bytes=24 << 20),
        cost_estimate=COST,
        name="prepare",
    )(device, ranks, transfer)


def own_kernel(index, span, weights_ref, mine_ref, out_ref):
    high, low = split(mine_ref[:, span])
    terms = jnp.concatenate([high, low, high], axis=0)
    out_ref[...] = jnp.dot(
        weights_ref[index, :, : terms.shape[0]], terms, preferred_element_type=jnp.float32
    )


def other_kernel(index, span, weights_ref, own_ref, got_ref, out_ref):
    high, low = split(got_ref[:, span])
    terms = jnp.concatenate([high, low, high], axis=0)
    out_ref[...] = own_ref[...] + jnp.dot(
        weights_ref[index, :, terms.shape[0] :], terms, preferred_element_type=jnp.float32
    )


def mix(kernel, index, start, count, *operands):
    width = operands[-1].shape[0]
    return pl.pallas_call(
        functools.partial(kernel, index, slice(start, start + count)),
        in_specs=[VMEM] * len(operands),
        out_specs=VMEM,
        out_shape=jax.ShapeDtypeStruct((width, count), jnp.float32),
        compiler_params=pltpu.CompilerParams(vmem_limit_bytes=16 << 20),
        cost_estimate=COST,
        name="mix",
    )(*operands)


def per_device(coefficients, transfer, ranks):
    levels = transfer.shape[0]
    place = lax.axis_index(("grp", "node"))
    devices = lax.axis_size(("grp", "node"))
    device = place.astype(jnp.int32)[None]
    starts = [sum(WIDTHS[:i]) for i in range(len(WIDTHS))]

    def exchange(values, level):
        pairs = [(i, i ^ 1 << level) for i in range(devices)]
        return lax.ppermute(values, ("grp", "node"), pairs)

    from_core = exchange(coefficients, 0)
    weights = prepare(device, ranks, transfer, 0, 1)
    state, partner = {}, {}
    last = None
    for chunk, level in ORDER:
        if level == 0:
            matrix, index, mine, got = weights, 0, coefficients, from_core
            start = starts[chunk]
        else:
            matrix, index, mine, got = later, level - 1, state[chunk], partner[chunk]
            start = 0
        if last is not None:
            mine, last = lax.optimization_barrier((mine, last))
        total = mix(own_kernel, index, start, WIDTHS[chunk], matrix, mine)
        got, total = lax.optimization_barrier((got, total))
        total = mix(other_kernel, index, start, WIDTHS[chunk], matrix, total, got)
        state[chunk] = last = total
        if level + 1 < levels:
            partner[chunk] = exchange(state[chunk], level + 1)
        if (chunk, level) == ORDER[0]:
            held, last = lax.optimization_barrier((ranks, last))
            later = prepare(device, held, transfer, 1, levels - 1)
    return jnp.concatenate([state[chunk] for chunk in range(len(WIDTHS))], axis=1)


def solution(mesh):
    return jax.shard_map(
        per_device,
        mesh=mesh,
        in_specs=(
            P(("grp", "node"), None),
            P(None, ("grp", "node"), None),
            P(None, ("grp", "node")),
        ),
        out_specs=P(("grp", "node"), None),
        check_vma=False,
    )
```

time: 176 us -> 165 us (0.938)
  Pallas kernels: 0 us -> 20.6 us
  matrix products: 18.4 us -> 0 us
  waiting for transfers between devices: 87.3 us -> 78.8 us
  other arithmetic: 9.4 us -> 1.09 us
  local copies, waits for them, and re-layouts: 1.84 us -> 5.81 us
    pallas_call x0 -> x66, Pallas kernels: none -> 20.6 us  [the longest x64 18.4 us: mix(): pl.pallas_call(functools.partial(kernel, index, slice(start, start + coun...]
    dot_general x64 -> x0, matrix products: 18.4 us -> none  [dot(): jnp.dot(a, b, precision=lax.Precision.HIGH, preferred_element_type=jnp.fl...]
    ppermute x29, waiting for transfers between devices: 87.3 us -> 78.8 us  [exchange(): return lax.ppermute(values, ('grp', 'node'), pairs)]
    unnamed x4 -> x13, local copies, waits for them, and re-layouts: 0.01 us -> 5.73 us
    lt x5 -> x0, other arithmetic: 5.25 us -> none  [halves(): matrix = jnp.where(rows < limits[level, 0], matrices[level], 0.0)]
    select_n x2 -> x0, other arithmetic: 2.06 us -> none  [halves(): matrix = jnp.where(rows < limits[level, 0], matrices[level], 0.0)]
    slice x2 -> x0, local copies, waits for them, and re-layouts: 1.83 us -> none  [the longest x1 1.17 us: columns(): return values[:, starts[chunk]:starts[chunk] + WIDTHS[chunk]]]
  transfers between devices with their start and end apart: 29 -> 29, of which waited for: 15 -> 16; matrix products, arithmetic and copies ran while one was open for 16% -> 0% of each run, Pallas kernels for 0% -> 12%
where the time goes in v2:
time: 165 us; the launch traced here: 164 us
  waiting for transfers between devices  78.8 us (48%)
  starting transfers between devices  57.5 us (35%)
  Pallas kernels  20.6 us (12%)
  local copies, waits for them, and re-layouts  5.81 us (4%)
    ppermute x29, waiting for transfers between devices, exchange(): return lax.ppermute(values, ('grp', 'node'), pairs)  78.8 us
    ppermute x29, starting transfers between devices, exchange(): return lax.ppermute(values, ('grp', 'node'), pairs)  57.5 us
    pallas_call x64, Pallas kernels, mix(): pl.pallas_call(functools.partial(kernel, index, slice(start, start + coun...  18.4 us
    unnamed x13, local copies, waits for them, and re-layouts  5.73 us
  transfers between devices with their start and end apart: 29, of which 16 were waited for; matrix products, arithmetic and copies ran while one was open for 0% of the time, Pallas kernels for 12%

profile of v2, /device:TPU:8, one launch (start us, length us, event | category | flops | bytes accessed | tf_op | source)
XLA Modules:
  0.0 164.4 jit_solution(14462620863239079474)
XLA Ops:
  0.0 0.7 copy.4.ranks_ref
  0.7 2.2 %copy-done = f32[8,256,512]{2,1,0:T(8,128)S(1)} copy-done((f32[8,256,512]{2,1,0:T(8,128)S(1)}, f32[8,256,512]{2,1,0:T(8,128)}, u32[]{:S(2)}) %copy-start) | copy-done | bytes 4194328
  2.9 0.7 prepare.2.weights_ref
  3.6 0.5 copy-done.2
  4.1 0.4 mix.64.own_ref
  4.5 0.4 mix.65.mine_ref
  5.0 1.9 %collective-permute-start.1 = (f32[256,384]{1,0:T(8,128)S(1)}, f32[256,384]{1,0:T(8,128)S(1)}, u32[]{:S(2)}, u32[]{:S(2)}) collective-permute-start(f32[256,384]{1,0:T(8,128)S(1)} %mix.65.mine_ref), channel_id=1, source_target_pairs={{0,2},{1,3},{2,0},{3,1},{4,6},{5,7},{6,4},{7,5},{8,10},{9,11},{10,... | collective-permute-start | bytes 1179656 | tf_op jit(solution)/shard_map/ppermute | solution.py:90
  7.0 2.2 %copy-done.1 = f32[8,256,512]{2,1,0:T(8,128)S(1)} copy-done((f32[8,256,512]{2,1,0:T(8,128)S(1)}, f32[8,256,512]{2,1,0:T(8,128)}, u32[]{:S(2)}) %copy-start.1) | copy-done | bytes 4194328
  9.2 1.5 prepare.3.weights_ref
  10.7 0.4 mix.66.own_ref
  11.1 5.6 %collective-permute-done.1.got_ref = f32[256,384]{1,0:T(8,128)S(1)} collective-permute-done((f32[256,384]{1,0:T(8,128)S(1)}, f32[256,384]{1,0:T(8,128)S(1)}, u32[]{:S(2)}, u32[]{:S(2)}) %collective-permute-start.1) | collective-permute-done | bytes 393248 | tf_op jit(solution)/shard_map/ppermute | solution.py:90
  16.7 0.4 mix.67.mine_ref
  17.1 3.4 %collective-permute-start.2 = (f32[256,384]{1,0:T(8,128)S(1)}, f32[256,384]{1,0:T(8,128)S(1)}, u32[]{:S(2)}, u32[]{:S(2)}) collective-permute-start(f32[256,384]{1,0:T(8,128)S(1)} %mix.67.mine_ref), channel_id=1, source_target_pairs={{0,4},{1,5},{2,6},{3,7},{4,0},{5,1},{6,2},{7,3},{8,12},{9,13},{10,... | collective-permute-start | bytes 1179656 | tf_op jit(solution)/shard_map/ppermute | solution.py:90
  21.0 1.8 %collective-permute-start.4 = (f32[256,256]{1,0:T(8,128)S(1)}, f32[256,256]{1,0:T(8,128)S(1)}, u32[]{:S(2)}, u32[]{:S(2)}) collective-permute-start(f32[256,256]{1,0:T(8,128)S(1)} %mix.69.mine_ref), channel_id=1, source_target_pairs={{0,2},{1,3},{2,0},{3,1},{4,6},{5,7},{6,4},{7,5},{8,10},{9,11},{10,... | collective-permute-start | bytes 786440 | tf_op jit(solution)/shard_map/ppermute | solution.py:90
  22.8 0.4 mix.70.own_ref
  23.2 14.8 %collective-permute-done.2.got_ref = f32[256,384]{1,0:T(8,128)S(1)} collective-permute-done((f32[256,384]{1,0:T(8,128)S(1)}, f32[256,384]{1,0:T(8,128)S(1)}, u32[]{:S(2)}, u32[]{:S(2)}) %collective-permute-start.2) | collective-permute-done | bytes 393248 | tf_op jit(solution)/shard_map/ppermute | solution.py:90
  38.0 0.4 mix.71.mine_ref
  39.0 6.4 %collective-permute-start.3 = (f32[256,384]{1,0:T(8,128)S(1)}, f32[256,384]{1,0:T(8,128)S(1)}, u32[]{:S(2)}, u32[]{:S(2)}) collective-permute-start(f32[256,384]{1,0:T(8,128)S(1)} %mix.71.mine_ref), channel_id=1, source_target_pairs={{0,8},{1,9},{2,10},{3,11},{4,12},{5,13},{6,14},{7,15},{8,0},{9,1},... | collective-permute-start | bytes 1179656 | tf_op jit(solution)/shard_map/ppermute | solution.py:90
  46.0 2.5 %collective-permute-start.7 = (f32[256,256]{1,0:T(8,128)S(1)}, f32[256,256]{1,0:T(8,128)S(1)}, u32[]{:S(2)}, u32[]{:S(2)}) collective-permute-start(f32[256,256]{1,0:T(8,128)S(1)} %mix.75.mine_ref), channel_id=1, source_target_pairs={{0,2},{1,3},{2,0},{3,1},{4,6},{5,7},{6,4},{7,5},{8,10},{9,11},{10,... | collective-permute-start | bytes 786440 | tf_op jit(solution)/shard_map/ppermute | solution.py:90
  48.7 21.2 %collective-permute-done.5.got_ref = f32[256,256]{1,0:T(8,128)S(1)} collective-permute-done((f32[256,256]{1,0:T(8,128)S(1)}, f32[256,256]{1,0:T(8,128)S(1)}, u32[]{:S(2)}, u32[]{:S(2)}) %collective-permute-start.5) | collective-permute-done | bytes 262176 | tf_op jit(solution)/shard_map/ppermute | solution.py:90
  70.1 6.0 %collective-permute-start.9 = (f32[256,256]{1,0:T(8,128)S(1)}, f32[256,256]{1,0:T(8,128)S(1)}, u32[]{:S(2)}, u32[]{:S(2)}) collective-permute-start(f32[256,256]{1,0:T(8,128)S(1)} %mix.77.mine_ref), channel_id=1, source_target_pairs={{0,8},{1,9},{2,10},{3,11},{4,12},{5,13},{6,14},{7,15},{8,0},{9,1},... | collective-permute-start | bytes 786440 | tf_op jit(solution)/shard_map/ppermute | solution.py:90
  76.1 0.4 mix.78.own_ref
  76.5 0.4 mix.79.mine_ref
  76.9 3.1 %collective-permute-start.6 = (f32[256,384]{1,0:T(8,128)S(1)}, f32[256,384]{1,0:T(8,128)S(1)}, u32[]{:S(2)}, u32[]{:S(2)}) collective-permute-start(f32[256,384]{1,0:T(8,128)S(1)} %mix.79.mine_ref), channel_id=1, source_target_pairs={{0,16},{1,17},{2,18},{3,19},{4,20},{5,21},{6,22},{7,23},{8,24},{9,... | collective-permute-start | bytes 1179656 | tf_op jit(solution)/shard_map/ppermute | solution.py:90
  81.2 1.9 %collective-permute-start.11 = (f32[256,256]{1,0:T(8,128)S(1)}, f32[256,256]{1,0:T(8,128)S(1)}, u32[]{:S(2)}, u32[]{:S(2)}) collective-permute-start(f32[256,256]{1,0:T(8,128)S(1)} %mix.83.mine_ref), channel_id=1, source_target_pairs={{0,4},{1,5},{2,6},{3,7},{4,0},{5,1},{6,2},{7,3},{8,12},{9,13},{10,... | collective-permute-start | bytes 786440 | tf_op jit(solution)/shard_map/ppermute | solution.py:90
  83.1 0.4 mix.84.own_ref
  83.5 5.7 %collective-permute-done.6.got_ref = f32[256,384]{1,0:T(8,128)S(1)} collective-permute-done((f32[256,384]{1,0:T(8,128)S(1)}, f32[256,384]{1,0:T(8,128)S(1)}, u32[]{:S(2)}, u32[]{:S(2)}) %collective-permute-start.6) | collective-permute-done | bytes 393248 | tf_op jit(solution)/shard_map/ppermute | solution.py:90
  89.2 0.4 mix.85.mine_ref
  90.1 3.1 %collective-permute-start.10 = (f32[256,256]{1,0:T(8,128)S(1)}, f32[256,256]{1,0:T(8,128)S(1)}, u32[]{:S(2)}, u32[]{:S(2)}) collective-permute-start(f32[256,256]{1,0:T(8,128)S(1)} %mix.87.mine_ref), channel_id=1, source_target_pairs={{0,16},{1,17},{2,18},{3,19},{4,20},{5,21},{6,22},{7,23},{8,24},{9,... | collective-permute-start | bytes 786440 | tf_op jit(solution)/shard_map/ppermute | solution.py:90
  93.2 0.6 collective-permute-start.8
  94.6 4.7 %collective-permute-done.11.got_ref = f32[256,256]{1,0:T(8,128)S(1)} collective-permute-done((f32[256,256]{1,0:T(8,128)S(1)}, f32[256,256]{1,0:T(8,128)S(1)}, u32[]{:S(2)}, u32[]{:S(2)}) %collective-permute-start.11) | collective-permute-done | bytes 262176 | tf_op jit(solution)/shard_map/ppermute | solution.py:90
  99.6 1.4 collective-permute-start.15
  101.0 1.5 collective-permute-start.14
  103.1 1.5 collective-permute-start.16
  104.6 0.4 mix.94.own_ref
  105.0 4.5 %collective-permute-done.8.got_ref = f32[256,384]{1,0:T(8,128)S(1)} collective-permute-done((f32[256,384]{1,0:T(8,128)S(1)}, f32[256,384]{1,0:T(8,128)S(1)}, u32[]{:S(2)}, u32[]{:S(2)}) %collective-permute-start.8) | collective-permute-done | bytes 393248 | tf_op jit(solution)/shard_map/ppermute | solution.py:90
  109.5 0.4 mix.95.mine_ref
  109.8 0.3 collective-permute-start.13
  110.4 2.4 %collective-permute-done.16.got_ref = f32[256,256]{1,0:T(8,128)S(1)} collective-permute-done((f32[256,256]{1,0:T(8,128)S(1)}, f32[256,256]{1,0:T(8,128)S(1)}, u32[]{:S(2)}, u32[]{:S(2)}) %collective-permute-start.16) | collective-permute-done | bytes 262176 | tf_op jit(solution)/shard_map/ppermute | solution.py:90
  113.4 2.3 %collective-permute-done.15.got_ref = f32[256,256]{1,0:T(8,128)S(1)} collective-permute-done((f32[256,256]{1,0:T(8,128)S(1)}, f32[256,256]{1,0:T(8,128)S(1)}, u32[]{:S(2)}, u32[]{:S(2)}) %collective-permute-start.15) | collective-permute-done | bytes 262176 | tf_op jit(solution)/shard_map/ppermute | solution.py:90
  115.9 3.0 %collective-permute-start.20 = (f32[256,256]{1,0:T(8,128)S(1)}, f32[256,256]{1,0:T(8,128)S(1)}, u32[]{:S(2)}, u32[]{:S(2)}) collective-permute-start(f32[256,256]{1,0:T(8,128)S(1)} %mix.99.mine_ref), channel_id=1, source_target_pairs={{0,16},{1,17},{2,18},{3,19},{4,20},{5,21},{6,22},{7,23},{8,24},{9,... | collective-permute-start | bytes 786440 | tf_op jit(solution)/shard_map/ppermute | solution.py:90
  119.0 0.5 collective-permute-start.19
  119.7 0.7 collective-permute-done.14.got_ref
  120.6 3.6 %collective-permute-start.18 = (f32[256,128]{1,0:T(8,128)S(1)}, f32[256,128]{1,0:T(8,128)S(1)}, u32[]{:S(2)}, u32[]{:S(2)}) collective-permute-start(f32[256,128]{1,0:T(8,128)S(1)} %mix.101.mine_ref), channel_id=1, source_target_pairs={{0,8},{1,9},{2,10},{3,11},{4,12},{5,13},{6,14},{7,15},{8,0},{9,1},... | collective-permute-start | bytes 393224 | tf_op jit(solution)/shard_map/ppermute | solution.py:90
  124.2 0.4 mix.102.own_ref
  124.6 0.4 mix.103.mine_ref
  125.0 2.7 %collective-permute-start.17 = (f32[256,384]{1,0:T(8,128)S(1)}, f32[256,384]{1,0:T(8,128)S(1)}, u32[]{:S(2)}, u32[]{:S(2)}) collective-permute-start(f32[256,384]{1,0:T(8,128)S(1)} %mix.103.mine_ref), channel_id=1, source_target_pairs={{0,128},{1,129},{2,130},{3,131},{4,132},{5,133},{6,134},{7,135},{8... | collective-permute-start | bytes 1179656 | tf_op jit(solution)/shard_map/ppermute | solution.py:90
  128.2 1.1 collective-permute-start.23
  130.1 2.7 %collective-permute-done.18.got_ref = f32[256,128]{1,0:T(8,128)S(1)} collective-permute-done((f32[256,128]{1,0:T(8,128)S(1)}, f32[256,128]{1,0:T(8,128)S(1)}, u32[]{:S(2)}, u32[]{:S(2)}) %collective-permute-start.18) | collective-permute-done | bytes 131104 | tf_op jit(solution)/shard_map/ppermute | solution.py:90
  133.0 3.1 %collective-permute-start.22 = (f32[256,128]{1,0:T(8,128)S(1)}, f32[256,128]{1,0:T(8,128)S(1)}, u32[]{:S(2)}, u32[]{:S(2)}) collective-permute-start(f32[256,128]{1,0:T(8,128)S(1)} %mix.109.mine_ref), channel_id=1, source_target_pairs={{0,16},{1,17},{2,18},{3,19},{4,20},{5,21},{6,22},{7,23},{8,24},{9,... | collective-permute-start | bytes 393224 | tf_op jit(solution)/shard_map/ppermute | solution.py:90
  136.1 2.3 %collective-permute-start.21 = (f32[256,256]{1,0:T(8,128)S(1)}, f32[256,256]{1,0:T(8,128)S(1)}, u32[]{:S(2)}, u32[]{:S(2)}) collective-permute-start(f32[256,256]{1,0:T(8,128)S(1)} %mix.107.mine_ref), channel_id=1, source_target_pairs={{0,128},{1,129},{2,130},{3,131},{4,132},{5,133},{6,134},{7,135},{8... | collective-permute-start | bytes 786440 | tf_op jit(solution)/shard_map/ppermute | solution.py:90
  138.4 0.4 mix.110.own_ref
  138.8 0.4 mix.111
  140.0 0.5 collective-permute-done.22.got_ref
  140.7 1.1 collective-permute-start.24
  141.9 0.5 collective-permute-start.25
  142.6 3.2 %collective-permute-done.24.got_ref = f32[256,128]{1,0:T(8,128)S(1)} collective-permute-done((f32[256,128]{1,0:T(8,128)S(1)}, f32[256,128]{1,0:T(8,128)S(1)}, u32[]{:S(2)}, u32[]{:S(2)}) %collective-permute-start.24) | collective-permute-done | bytes 131104 | tf_op jit(solution)/shard_map/ppermute | solution.py:90
  146.1 1.4 collective-permute-start.27
  148.3 4.3 %collective-permute-done.25.got_ref = f32[256,256]{1,0:T(8,128)S(1)} collective-permute-done((f32[256,256]{1,0:T(8,128)S(1)}, f32[256,256]{1,0:T(8,128)S(1)}, u32[]{:S(2)}, u32[]{:S(2)}) %collective-permute-start.25) | collective-permute-done | bytes 262176 | tf_op jit(solution)/shard_map/ppermute | solution.py:90
  153.3 1.2 collective-permute-done.27.got_ref
  154.7 2.3 %collective-permute-start.28 = (f32[256,128]{1,0:T(8,128)S(1)}, f32[256,128]{1,0:T(8,128)S(1)}, u32[]{:S(2)}, u32[]{:S(2)}) collective-permute-start(f32[256,128]{1,0:T(8,128)S(1)} %mix.123.mine_ref), channel_id=1, source_target_pairs={{0,128},{1,129},{2,130},{3,131},{4,132},{5,133},{6,134},{7,135},{8... | collective-permute-start | bytes 393224 | tf_op jit(solution)/shard_map/ppermute | solution.py:90
  157.3 4.3 %collective-permute-done.26.got_ref = f32[256,256]{1,0:T(8,128)S(1)} collective-permute-done((f32[256,256]{1,0:T(8,128)S(1)}, f32[256,256]{1,0:T(8,128)S(1)}, u32[]{:S(2)}, u32[]{:S(2)}) %collective-permute-start.26) | collective-permute-done | bytes 262176 | tf_op jit(solution)/shard_map/ppermute | solution.py:90
  162.2 0.9 collective-permute-done.28.got_ref
  163.3 1.1 pad_maximum_fusion
  (75 shorter events, 13.1 us)
Async XLA Ops:
  0.0 4.5 %collective-permute-start = (f32[256,1024]{1,0:T(8,128)}, f32[256,1024]{1,0:T(8,128)S(1)}, u32[]{:S(2)}, u32[]{:S(2)}) collective-permute-start(f32[256,1024]{1,0:T(8,128)} %mine_ref.4), channel_id=1, source_target_pairs={{0,1},{1,0},{2,3},{3,2},{4,5},{5,4},{6,7},{7,6},{8,9},{9,8},{10,11... | collective-permute-start | bytes 3145736 | tf_op jit(solution)/shard_map/ppermute | solution.py:90
  0.7 2.2 %copy-start = (f32[8,256,512]{2,1,0:T(8,128)S(1)}, f32[8,256,512]{2,1,0:T(8,128)}, u32[]{:S(2)}) copy-start(f32[8,256,512]{2,1,0:T(8,128)} %matrix_ref.3) | copy-start | bytes 12582916
  2.9 1.2 copy-start.2
  4.1 0.9 copy-start.3
  4.5 2.4 %copy-start.5 = (s32[8,1]{0,1:T(1,128)S(1)}, s32[8,1]{0,1:T(1,128)}, u32[]{:S(2)}) copy-start(s32[8,1]{0,1:T(1,128)} %param.5) | copy-start | bytes 100
  5.0 11.7 %collective-permute-start.1 = (f32[256,384]{1,0:T(8,128)S(1)}, f32[256,384]{1,0:T(8,128)S(1)}, u32[]{:S(2)}, u32[]{:S(2)}) collective-permute-start(f32[256,384]{1,0:T(8,128)S(1)} %mix.65.mine_ref), channel_id=1, source_target_pairs={{0,2},{1,3},{2,0},{3,1},{4,6},{5,7},{6,4},{7,5},{8,10},{9,11},{10,... | collective-permute-start | bytes 1179656 | tf_op jit(solution)/shard_map/ppermute | solution.py:90
  7.0 2.2 %copy-start.1 = (f32[8,256,512]{2,1,0:T(8,128)S(1)}, f32[8,256,512]{2,1,0:T(8,128)}, u32[]{:S(2)}) copy-start(f32[8,256,512]{2,1,0:T(8,128)} %matrix_ref.3) | copy-start | bytes 12582916
  11.1 9.4 %copy-start.4 = (bf16[1,256,1536]{2,1,0:T(8,128)(2,1)S(1)}, bf16[1,256,1536]{2,1,0:T(8,128)(2,1)}, u32[]{:S(2)}) copy-start(bf16[1,256,1536]{2,1,0:T(8,128)(2,1)} %copy-done.3) | copy-start | bytes 2359300
  17.1 20.9 %collective-permute-start.2 = (f32[256,384]{1,0:T(8,128)S(1)}, f32[256,384]{1,0:T(8,128)S(1)}, u32[]{:S(2)}, u32[]{:S(2)}) collective-permute-start(f32[256,384]{1,0:T(8,128)S(1)} %mix.67.mine_ref), channel_id=1, source_target_pairs={{0,4},{1,5},{2,6},{3,7},{4,0},{5,1},{6,2},{7,3},{8,12},{9,13},{10,... | collective-permute-start | bytes 1179656 | tf_op jit(solution)/shard_map/ppermute | solution.py:90
  21.0 17.6 %collective-permute-start.4 = (f32[256,256]{1,0:T(8,128)S(1)}, f32[256,256]{1,0:T(8,128)S(1)}, u32[]{:S(2)}, u32[]{:S(2)}) collective-permute-start(f32[256,256]{1,0:T(8,128)S(1)} %mix.69.mine_ref), channel_id=1, source_target_pairs={{0,2},{1,3},{2,0},{3,1},{4,6},{5,7},{6,4},{7,5},{8,10},{9,11},{10,... | collective-permute-start | bytes 786440 | tf_op jit(solution)/shard_map/ppermute | solution.py:90
  38.9 30.9 %collective-permute-start.5 = (f32[256,256]{1,0:T(8,128)S(1)}, f32[256,256]{1,0:T(8,128)S(1)}, u32[]{:S(2)}, u32[]{:S(2)}) collective-permute-start(f32[256,256]{1,0:T(8,128)S(1)} %mix.73.mine_ref), channel_id=1, source_target_pairs={{0,4},{1,5},{2,6},{3,7},{4,0},{5,1},{6,2},{7,3},{8,12},{9,13},{10,... | collective-permute-start | bytes 786440 | tf_op jit(solution)/shard_map/ppermute | solution.py:90
  39.0 37.5 %collective-permute-start.3 = (f32[256,384]{1,0:T(8,128)S(1)}, f32[256,384]{1,0:T(8,128)S(1)}, u32[]{:S(2)}, u32[]{:S(2)}) collective-permute-start(f32[256,384]{1,0:T(8,128)S(1)} %mix.71.mine_ref), channel_id=1, source_target_pairs={{0,8},{1,9},{2,10},{3,11},{4,12},{5,13},{6,14},{7,15},{8,0},{9,1},... | collective-permute-start | bytes 1179656 | tf_op jit(solution)/shard_map/ppermute | solution.py:90
  46.0 34.9 %collective-permute-start.7 = (f32[256,256]{1,0:T(8,128)S(1)}, f32[256,256]{1,0:T(8,128)S(1)}, u32[]{:S(2)}, u32[]{:S(2)}) collective-permute-start(f32[256,256]{1,0:T(8,128)S(1)} %mix.75.mine_ref), channel_id=1, source_target_pairs={{0,2},{1,3},{2,0},{3,1},{4,6},{5,7},{6,4},{7,5},{8,10},{9,11},{10,... | collective-permute-start | bytes 786440 | tf_op jit(solution)/shard_map/ppermute | solution.py:90
  70.1 19.7 %collective-permute-start.9 = (f32[256,256]{1,0:T(8,128)S(1)}, f32[256,256]{1,0:T(8,128)S(1)}, u32[]{:S(2)}, u32[]{:S(2)}) collective-permute-start(f32[256,256]{1,0:T(8,128)S(1)} %mix.77.mine_ref), channel_id=1, source_target_pairs={{0,8},{1,9},{2,10},{3,11},{4,12},{5,13},{6,14},{7,15},{8,0},{9,1},... | collective-permute-start | bytes 786440 | tf_op jit(solution)/shard_map/ppermute | solution.py:90
  76.9 12.3 %collective-permute-start.6 = (f32[256,384]{1,0:T(8,128)S(1)}, f32[256,384]{1,0:T(8,128)S(1)}, u32[]{:S(2)}, u32[]{:S(2)}) collective-permute-start(f32[256,384]{1,0:T(8,128)S(1)} %mix.79.mine_ref), channel_id=1, source_target_pairs={{0,16},{1,17},{2,18},{3,19},{4,20},{5,21},{6,22},{7,23},{8,24},{9,... | collective-permute-start | bytes 1179656 | tf_op jit(solution)/shard_map/ppermute | solution.py:90
  80.5 13.6 %collective-permute-start.12 = (f32[256,128]{1,0:T(8,128)S(1)}, f32[256,128]{1,0:T(8,128)S(1)}, u32[]{:S(2)}, u32[]{:S(2)}) collective-permute-start(f32[256,128]{1,0:T(8,128)S(1)} %mix.81.mine_ref), channel_id=1, source_target_pairs={{0,2},{1,3},{2,0},{3,1},{4,6},{5,7},{6,4},{7,5},{8,10},{9,11},{10,... | collective-permute-start | bytes 393224 | tf_op jit(solution)/shard_map/ppermute | solution.py:90
  81.2 18.1 %collective-permute-start.11 = (f32[256,256]{1,0:T(8,128)S(1)}, f32[256,256]{1,0:T(8,128)S(1)}, u32[]{:S(2)}, u32[]{:S(2)}) collective-permute-start(f32[256,256]{1,0:T(8,128)S(1)} %mix.83.mine_ref), channel_id=1, source_target_pairs={{0,4},{1,5},{2,6},{3,7},{4,0},{5,1},{6,2},{7,3},{8,12},{9,13},{10,... | collective-permute-start | bytes 786440 | tf_op jit(solution)/shard_map/ppermute | solution.py:90
  90.1 12.7 %collective-permute-start.10 = (f32[256,256]{1,0:T(8,128)S(1)}, f32[256,256]{1,0:T(8,128)S(1)}, u32[]{:S(2)}, u32[]{:S(2)}) collective-permute-start(f32[256,256]{1,0:T(8,128)S(1)} %mix.87.mine_ref), channel_id=1, source_target_pairs={{0,16},{1,17},{2,18},{3,19},{4,20},{5,21},{6,22},{7,23},{8,24},{9,... | collective-permute-start | bytes 786440 | tf_op jit(solution)/shard_map/ppermute | solution.py:90
  93.2 16.2 %collective-permute-start.8 = (f32[256,384]{1,0:T(8,128)S(1)}, f32[256,384]{1,0:T(8,128)S(1)}, u32[]{:S(2)}, u32[]{:S(2)}) collective-permute-start(f32[256,384]{1,0:T(8,128)S(1)} %mix.85.mine_ref), channel_id=1, source_target_pairs={{0,32},{1,33},{2,34},{3,35},{4,36},{5,37},{6,38},{7,39},{8,40},{9,... | collective-permute-start | bytes 1179656 | tf_op jit(solution)/shard_map/ppermute | solution.py:90
  99.6 16.1 %collective-permute-start.15 = (f32[256,256]{1,0:T(8,128)S(1)}, f32[256,256]{1,0:T(8,128)S(1)}, u32[]{:S(2)}, u32[]{:S(2)}) collective-permute-start(f32[256,256]{1,0:T(8,128)S(1)} %mix.91.mine_ref), channel_id=1, source_target_pairs={{0,8},{1,9},{2,10},{3,11},{4,12},{5,13},{6,14},{7,15},{8,0},{9,1},... | collective-permute-start | bytes 786440 | tf_op jit(solution)/shard_map/ppermute | solution.py:90
  101.0 19.4 %collective-permute-start.14 = (f32[256,128]{1,0:T(8,128)S(1)}, f32[256,128]{1,0:T(8,128)S(1)}, u32[]{:S(2)}, u32[]{:S(2)}) collective-permute-start(f32[256,128]{1,0:T(8,128)S(1)} %mix.89.mine_ref), channel_id=1, source_target_pairs={{0,4},{1,5},{2,6},{3,7},{4,0},{5,1},{6,2},{7,3},{8,12},{9,13},{10,... | collective-permute-start | bytes 393224 | tf_op jit(solution)/shard_map/ppermute | solution.py:90
  103.1 9.7 %collective-permute-start.16 = (f32[256,256]{1,0:T(8,128)S(1)}, f32[256,256]{1,0:T(8,128)S(1)}, u32[]{:S(2)}, u32[]{:S(2)}) collective-permute-start(f32[256,256]{1,0:T(8,128)S(1)} %mix.93.mine_ref), channel_id=1, source_target_pairs={{0,32},{1,33},{2,34},{3,35},{4,36},{5,37},{6,38},{7,39},{8,40},{9,... | collective-permute-start | bytes 786440 | tf_op jit(solution)/shard_map/ppermute | solution.py:90
  109.8 14.8 %collective-permute-start.13 = (f32[256,384]{1,0:T(8,128)S(1)}, f32[256,384]{1,0:T(8,128)S(1)}, u32[]{:S(2)}, u32[]{:S(2)}) collective-permute-start(f32[256,384]{1,0:T(8,128)S(1)} %mix.95.mine_ref), channel_id=1, source_target_pairs={{0,64},{1,65},{2,66},{3,67},{4,68},{5,69},{6,70},{7,71},{8,72},{9,... | collective-permute-start | bytes 1179656 | tf_op jit(solution)/shard_map/ppermute | solution.py:90
  115.9 12.0 %collective-permute-start.20 = (f32[256,256]{1,0:T(8,128)S(1)}, f32[256,256]{1,0:T(8,128)S(1)}, u32[]{:S(2)}, u32[]{:S(2)}) collective-permute-start(f32[256,256]{1,0:T(8,128)S(1)} %mix.99.mine_ref), channel_id=1, source_target_pairs={{0,16},{1,17},{2,18},{3,19},{4,20},{5,21},{6,22},{7,23},{8,24},{9,... | collective-permute-start | bytes 786440 | tf_op jit(solution)/shard_map/ppermute | solution.py:90
  119.0 10.6 %collective-permute-start.19 = (f32[256,256]{1,0:T(8,128)S(1)}, f32[256,256]{1,0:T(8,128)S(1)}, u32[]{:S(2)}, u32[]{:S(2)}) collective-permute-start(f32[256,256]{1,0:T(8,128)S(1)} %mix.97.mine_ref), channel_id=1, source_target_pairs={{0,64},{1,65},{2,66},{3,67},{4,68},{5,69},{6,70},{7,71},{8,72},{9,... | collective-permute-start | bytes 786440 | tf_op jit(solution)/shard_map/ppermute | solution.py:90
  120.6 12.2 %collective-permute-start.18 = (f32[256,128]{1,0:T(8,128)S(1)}, f32[256,128]{1,0:T(8,128)S(1)}, u32[]{:S(2)}, u32[]{:S(2)}) collective-permute-start(f32[256,128]{1,0:T(8,128)S(1)} %mix.101.mine_ref), channel_id=1, source_target_pairs={{0,8},{1,9},{2,10},{3,11},{4,12},{5,13},{6,14},{7,15},{8,0},{9,1},... | collective-permute-start | bytes 393224 | tf_op jit(solution)/shard_map/ppermute | solution.py:90
  125.0 13.8 %collective-permute-start.17 = (f32[256,384]{1,0:T(8,128)S(1)}, f32[256,384]{1,0:T(8,128)S(1)}, u32[]{:S(2)}, u32[]{:S(2)}) collective-permute-start(f32[256,384]{1,0:T(8,128)S(1)} %mix.103.mine_ref), channel_id=1, source_target_pairs={{0,128},{1,129},{2,130},{3,131},{4,132},{5,133},{6,134},{7,135},{8... | collective-permute-start | bytes 1179656 | tf_op jit(solution)/shard_map/ppermute | solution.py:90
  128.2 11.2 %collective-permute-start.23 = (f32[256,256]{1,0:T(8,128)S(1)}, f32[256,256]{1,0:T(8,128)S(1)}, u32[]{:S(2)}, u32[]{:S(2)}) collective-permute-start(f32[256,256]{1,0:T(8,128)S(1)} %mix.105.mine_ref), channel_id=1, source_target_pairs={{0,32},{1,33},{2,34},{3,35},{4,36},{5,37},{6,38},{7,39},{8,40},{9,... | collective-permute-start | bytes 786440 | tf_op jit(solution)/shard_map/ppermute | solution.py:90
  133.0 7.5 %collective-permute-start.22 = (f32[256,128]{1,0:T(8,128)S(1)}, f32[256,128]{1,0:T(8,128)S(1)}, u32[]{:S(2)}, u32[]{:S(2)}) collective-permute-start(f32[256,128]{1,0:T(8,128)S(1)} %mix.109.mine_ref), channel_id=1, source_target_pairs={{0,16},{1,17},{2,18},{3,19},{4,20},{5,21},{6,22},{7,23},{8,24},{9,... | collective-permute-start | bytes 393224 | tf_op jit(solution)/shard_map/ppermute | solution.py:90
  136.1 11.6 %collective-permute-start.21 = (f32[256,256]{1,0:T(8,128)S(1)}, f32[256,256]{1,0:T(8,128)S(1)}, u32[]{:S(2)}, u32[]{:S(2)}) collective-permute-start(f32[256,256]{1,0:T(8,128)S(1)} %mix.107.mine_ref), channel_id=1, source_target_pairs={{0,128},{1,129},{2,130},{3,131},{4,132},{5,133},{6,134},{7,135},{8... | collective-permute-start | bytes 786440 | tf_op jit(solution)/shard_map/ppermute | solution.py:90
  140.7 5.1 %collective-permute-start.24 = (f32[256,128]{1,0:T(8,128)S(1)}, f32[256,128]{1,0:T(8,128)S(1)}, u32[]{:S(2)}, u32[]{:S(2)}) collective-permute-start(f32[256,128]{1,0:T(8,128)S(1)} %mix.115.mine_ref), channel_id=1, source_target_pairs={{0,32},{1,33},{2,34},{3,35},{4,36},{5,37},{6,38},{7,39},{8,40},{9,... | collective-permute-start | bytes 393224 | tf_op jit(solution)/shard_map/ppermute | solution.py:90
  141.9 10.7 %collective-permute-start.25 = (f32[256,256]{1,0:T(8,128)S(1)}, f32[256,256]{1,0:T(8,128)S(1)}, u32[]{:S(2)}, u32[]{:S(2)}) collective-permute-start(f32[256,256]{1,0:T(8,128)S(1)} %mix.113.mine_ref), channel_id=1, source_target_pairs={{0,64},{1,65},{2,66},{3,67},{4,68},{5,69},{6,70},{7,71},{8,72},{9,... | collective-permute-start | bytes 786440 | tf_op jit(solution)/shard_map/ppermute | solution.py:90
  146.1 8.4 %collective-permute-start.27 = (f32[256,128]{1,0:T(8,128)S(1)}, f32[256,128]{1,0:T(8,128)S(1)}, u32[]{:S(2)}, u32[]{:S(2)}) collective-permute-start(f32[256,128]{1,0:T(8,128)S(1)} %mix.117.mine_ref), channel_id=1, source_target_pairs={{0,64},{1,65},{2,66},{3,67},{4,68},{5,69},{6,70},{7,71},{8,72},{9,... | collective-permute-start | bytes 393224 | tf_op jit(solution)/shard_map/ppermute | solution.py:90
  152.9 8.8 %collective-permute-start.26 = (f32[256,256]{1,0:T(8,128)S(1)}, f32[256,256]{1,0:T(8,128)S(1)}, u32[]{:S(2)}, u32[]{:S(2)}) collective-permute-start(f32[256,256]{1,0:T(8,128)S(1)} %mix.121.mine_ref), channel_id=1, source_target_pairs={{0,128},{1,129},{2,130},{3,131},{4,132},{5,133},{6,134},{7,135},{8... | collective-permute-start | bytes 786440 | tf_op jit(solution)/shard_map/ppermute | solution.py:90
  154.7 8.3 %collective-permute-start.28 = (f32[256,128]{1,0:T(8,128)S(1)}, f32[256,128]{1,0:T(8,128)S(1)}, u32[]{:S(2)}, u32[]{:S(2)}) collective-permute-start(f32[256,128]{1,0:T(8,128)S(1)} %mix.123.mine_ref), channel_id=1, source_target_pairs={{0,128},{1,129},{2,130},{3,131},{4,132},{5,133},{6,134},{7,135},{8... | collective-permute-start | bytes 393224 | tf_op jit(solution)/shard_map/ppermute | solution.py:90

commit v3 on v2

--- a/solution.py
+++ b/solution.py
@@ -8,7 +8,7 @@
 from jax.sharding import PartitionSpec as P
 
 WIDTHS = (384, 256, 256, 128)
-ORDER = ((0, 0), (0, 1), (1, 0), (0, 2), (1, 1), (2, 0), (1, 2), (0, 3), (3, 0), (2, 1), (0, 4), (1, 3), (3, 1), (2, 2), (1, 4), (0, 5), (1, 5), (2, 3), (3, 2), (0, 6), (2, 4), (1, 6), (3, 3), (0, 7), (2, 5), (3, 4), (3, 5), (1, 7), (2, 6), (3, 6), (2, 7), (3, 7))
+ORDER = ((0, 0), (0, 1), (1, 0), (0, 2), (1, 1), (2, 0), (3, 0), (1, 2), (0, 3), (2, 1), (0, 4), (1, 3), (3, 1), (2, 2), (1, 4), (0, 5), (1, 5), (2, 3), (3, 2), (0, 6), (2, 4), (1, 6), (3, 3), (0, 7), (2, 5), (3, 4), (3, 5), (1, 7), (2, 6), (3, 6), (2, 7), (3, 7))
 VMEM = pl.BlockSpec(memory_space=pltpu.VMEM)
 SMEM = pl.BlockSpec(memory_space=pltpu.SMEM)
 COST = pl.CostEstimate(flops=2000000000, bytes_accessed=4000000, transcendentals=0)
@@ -25,7 +25,7 @@
     width = out_ref.shape[1]
     upper = device_ref[0] >> level & 1
     rows = lax.broadcasted_iota(jnp.int32, (width, width), 0)
-    keep = rows < ranks_ref[level, 0]
+    keep = rows < ranks_ref[0, level]
     for part in range(2):
         start = pl.multiple_of((upper ^ part) * width, width)
         half = jnp.where(keep, matrix_ref[0, :, pl.ds(start, width)], 0.0)
@@ -80,6 +80,7 @@
 
 def per_device(coefficients, transfer, ranks):
     levels = transfer.shape[0]
+    ranks = ranks.T
     place = lax.axis_index(("grp", "node"))
     devices = lax.axis_size(("grp", "node"))
     device = place.astype(jnp.int32)[None]

time: 165 us -> 164 us (level)
  waiting for transfers between devices: 78.8 us -> 85.4 us
  starting transfers between devices: 57.5 us -> 53.3 us
  local copies, waits for them, and re-layouts: 5.81 us -> 3.42 us
    ppermute x29, waiting for transfers between devices: 78.8 us -> 85.4 us  [exchange(): return lax.ppermute(values, ('grp', 'node'), pairs)]
    ppermute x29, starting transfers between devices: 57.5 us -> 53.3 us  [exchange(): return lax.ppermute(values, ('grp', 'node'), pairs)]
    unnamed x13 -> x6, local copies, waits for them, and re-layouts: 5.73 us -> 3.42 us
where the time goes in v3:
time: 164 us
  waiting for transfers between devices  85.4 us (52%)
  starting transfers between devices  53.3 us (32%)
  Pallas kernels  20.4 us (12%)
  local copies, waits for them, and re-layouts  3.42 us (2%)
    ppermute x29, waiting for transfers between devices, exchange(): return lax.ppermute(values, ('grp', 'node'), pairs)  85.4 us
    ppermute x29, starting transfers between devices, exchange(): return lax.ppermute(values, ('grp', 'node'), pairs)  53.3 us
    pallas_call x64, Pallas kernels, mix(): pl.pallas_call(functools.partial(kernel, index, slice(start, start + coun...  18.4 us
    unnamed x6, local copies, waits for them, and re-layouts  3.42 us
  transfers between devices with their start and end apart: 29, of which 16 were waited for; matrix products, arithmetic and copies ran while one was open for 0% of the time, Pallas kernels for 12%

profile of v3, /device:TPU:8, one launch (start us, length us, event | category | flops | bytes accessed | tf_op | source)
XLA Modules:
  0.0 164.3 jit_solution(11675153653754923372)
XLA Ops:
  0.0 2.2 %copy-done = f32[8,256,512]{2,1,0:T(8,128)S(1)} copy-done((f32[8,256,512]{2,1,0:T(8,128)S(1)}, f32[8,256,512]{2,1,0:T(8,128)}, u32[]{:S(2)}) %copy-start) | copy-done | bytes 4194328
  2.2 0.7 copy-done.1
  2.9 0.6 prepare.2.weights_ref
  3.5 0.6 copy-done.2
  4.1 0.4 mix.64.own_ref
  4.5 0.4 mix.65.mine_ref
  4.8 2.0 %collective-permute-start.1 = (f32[256,384]{1,0:T(8,128)S(1)}, f32[256,384]{1,0:T(8,128)S(1)}, u32[]{:S(2)}, u32[]{:S(2)}) collective-permute-start(f32[256,384]{1,0:T(8,128)S(1)} %mix.65.mine_ref), channel_id=1, source_target_pairs={{0,2},{1,3},{2,0},{3,1},{4,6},{5,7},{6,4},{7,5},{8,10},{9,11},{10,... | collective-permute-start | bytes 1179656 | tf_op jit(solution)/shard_map/ppermute | solution.py:91
  6.8 1.4 prepare.3.weights_ref
  8.3 0.4 mix.66.own_ref
  8.7 8.0 %collective-permute-done.1.got_ref = f32[256,384]{1,0:T(8,128)S(1)} collective-permute-done((f32[256,384]{1,0:T(8,128)S(1)}, f32[256,384]{1,0:T(8,128)S(1)}, u32[]{:S(2)}, u32[]{:S(2)}) %collective-permute-start.1) | collective-permute-done | bytes 393248 | tf_op jit(solution)/shard_map/ppermute | solution.py:91
  16.6 0.4 mix.67.mine_ref
  17.0 3.4 %collective-permute-start.2 = (f32[256,384]{1,0:T(8,128)S(1)}, f32[256,384]{1,0:T(8,128)S(1)}, u32[]{:S(2)}, u32[]{:S(2)}) collective-permute-start(f32[256,384]{1,0:T(8,128)S(1)} %mix.67.mine_ref), channel_id=1, source_target_pairs={{0,4},{1,5},{2,6},{3,7},{4,0},{5,1},{6,2},{7,3},{8,12},{9,13},{10,... | collective-permute-start | bytes 1179656 | tf_op jit(solution)/shard_map/ppermute | solution.py:91
  20.6 0.3 mix.69.mine_ref
  20.9 1.8 %collective-permute-start.4 = (f32[256,256]{1,0:T(8,128)S(1)}, f32[256,256]{1,0:T(8,128)S(1)}, u32[]{:S(2)}, u32[]{:S(2)}) collective-permute-start(f32[256,256]{1,0:T(8,128)S(1)} %mix.69.mine_ref), channel_id=1, source_target_pairs={{0,2},{1,3},{2,0},{3,1},{4,6},{5,7},{6,4},{7,5},{8,10},{9,11},{10,... | collective-permute-start | bytes 786440 | tf_op jit(solution)/shard_map/ppermute | solution.py:91
  22.7 0.4 mix.70.own_ref
  23.1 14.8 %collective-permute-done.2.got_ref = f32[256,384]{1,0:T(8,128)S(1)} collective-permute-done((f32[256,384]{1,0:T(8,128)S(1)}, f32[256,384]{1,0:T(8,128)S(1)}, u32[]{:S(2)}, u32[]{:S(2)}) %collective-permute-start.2) | collective-permute-done | bytes 393248 | tf_op jit(solution)/shard_map/ppermute | solution.py:91
  37.9 0.4 mix.71.mine_ref
  38.9 6.4 %collective-permute-start.3 = (f32[256,384]{1,0:T(8,128)S(1)}, f32[256,384]{1,0:T(8,128)S(1)}, u32[]{:S(2)}, u32[]{:S(2)}) collective-permute-start(f32[256,384]{1,0:T(8,128)S(1)} %mix.71.mine_ref), channel_id=1, source_target_pairs={{0,8},{1,9},{2,10},{3,11},{4,12},{5,13},{6,14},{7,15},{8,0},{9,1},... | collective-permute-start | bytes 1179656 | tf_op jit(solution)/shard_map/ppermute | solution.py:91
  45.6 0.3 mix.75.mine_ref
  45.8 2.5 %collective-permute-start.7 = (f32[256,256]{1,0:T(8,128)S(1)}, f32[256,256]{1,0:T(8,128)S(1)}, u32[]{:S(2)}, u32[]{:S(2)}) collective-permute-start(f32[256,256]{1,0:T(8,128)S(1)} %mix.75.mine_ref), channel_id=1, source_target_pairs={{0,2},{1,3},{2,0},{3,1},{4,6},{5,7},{6,4},{7,5},{8,10},{9,11},{10,... | collective-permute-start | bytes 786440 | tf_op jit(solution)/shard_map/ppermute | solution.py:91
  49.2 20.6 %collective-permute-done.5.got_ref = f32[256,256]{1,0:T(8,128)S(1)} collective-permute-done((f32[256,256]{1,0:T(8,128)S(1)}, f32[256,256]{1,0:T(8,128)S(1)}, u32[]{:S(2)}, u32[]{:S(2)}) %collective-permute-start.5) | collective-permute-done | bytes 262176 | tf_op jit(solution)/shard_map/ppermute | solution.py:91
  70.0 6.0 %collective-permute-start.9 = (f32[256,256]{1,0:T(8,128)S(1)}, f32[256,256]{1,0:T(8,128)S(1)}, u32[]{:S(2)}, u32[]{:S(2)}) collective-permute-start(f32[256,256]{1,0:T(8,128)S(1)} %mix.79.mine_ref), channel_id=1, source_target_pairs={{0,8},{1,9},{2,10},{3,11},{4,12},{5,13},{6,14},{7,15},{8,0},{9,1},... | collective-permute-start | bytes 786440 | tf_op jit(solution)/shard_map/ppermute | solution.py:91
  76.0 0.4 mix.80.own_ref
  76.4 0.4 mix.81.mine_ref
  76.8 3.1 %collective-permute-start.6 = (f32[256,384]{1,0:T(8,128)S(1)}, f32[256,384]{1,0:T(8,128)S(1)}, u32[]{:S(2)}, u32[]{:S(2)}) collective-permute-start(f32[256,384]{1,0:T(8,128)S(1)} %mix.81.mine_ref), channel_id=1, source_target_pairs={{0,16},{1,17},{2,18},{3,19},{4,20},{5,21},{6,22},{7,23},{8,24},{9,... | collective-permute-start | bytes 1179656 | tf_op jit(solution)/shard_map/ppermute | solution.py:91
  80.4 0.3 collective-permute-start.11
  80.7 0.4 mix.84.own_ref
  81.1 8.0 %collective-permute-done.6.got_ref = f32[256,384]{1,0:T(8,128)S(1)} collective-permute-done((f32[256,384]{1,0:T(8,128)S(1)}, f32[256,384]{1,0:T(8,128)S(1)}, u32[]{:S(2)}, u32[]{:S(2)}) %collective-permute-start.6) | collective-permute-done | bytes 393248 | tf_op jit(solution)/shard_map/ppermute | solution.py:91
  89.1 0.4 mix.85.mine_ref
  90.0 3.1 %collective-permute-start.10 = (f32[256,256]{1,0:T(8,128)S(1)}, f32[256,256]{1,0:T(8,128)S(1)}, u32[]{:S(2)}, u32[]{:S(2)}) collective-permute-start(f32[256,256]{1,0:T(8,128)S(1)} %mix.87.mine_ref), channel_id=1, source_target_pairs={{0,16},{1,17},{2,18},{3,19},{4,20},{5,21},{6,22},{7,23},{8,24},{9,... | collective-permute-start | bytes 786440 | tf_op jit(solution)/shard_map/ppermute | solution.py:91
  93.1 0.6 collective-permute-start.8
  94.5 5.7 %collective-permute-done.11.got_ref = f32[256,256]{1,0:T(8,128)S(1)} collective-permute-done((f32[256,256]{1,0:T(8,128)S(1)}, f32[256,256]{1,0:T(8,128)S(1)}, u32[]{:S(2)}, u32[]{:S(2)}) %collective-permute-start.11) | collective-permute-done | bytes 262176 | tf_op jit(solution)/shard_map/ppermute | solution.py:91
  100.4 0.9 collective-permute-start.15
  101.9 1.6 collective-permute-start.16
  103.5 0.4 mix.94.own_ref
  103.8 5.5 %collective-permute-done.8.got_ref = f32[256,384]{1,0:T(8,128)S(1)} collective-permute-done((f32[256,384]{1,0:T(8,128)S(1)}, f32[256,384]{1,0:T(8,128)S(1)}, u32[]{:S(2)}, u32[]{:S(2)}) %collective-permute-start.8) | collective-permute-done | bytes 393248 | tf_op jit(solution)/shard_map/ppermute | solution.py:91
  109.3 0.4 mix.95.mine_ref
  109.7 0.3 collective-permute-start.13
  110.3 2.4 %collective-permute-done.16.got_ref = f32[256,256]{1,0:T(8,128)S(1)} collective-permute-done((f32[256,256]{1,0:T(8,128)S(1)}, f32[256,256]{1,0:T(8,128)S(1)}, u32[]{:S(2)}, u32[]{:S(2)}) %collective-permute-start.16) | collective-permute-done | bytes 262176 | tf_op jit(solution)/shard_map/ppermute | solution.py:91
  113.3 3.2 %collective-permute-done.15.got_ref = f32[256,256]{1,0:T(8,128)S(1)} collective-permute-done((f32[256,256]{1,0:T(8,128)S(1)}, f32[256,256]{1,0:T(8,128)S(1)}, u32[]{:S(2)}, u32[]{:S(2)}) %collective-permute-start.15) | collective-permute-done | bytes 262176 | tf_op jit(solution)/shard_map/ppermute | solution.py:91
  116.7 3.1 %collective-permute-start.20 = (f32[256,256]{1,0:T(8,128)S(1)}, f32[256,256]{1,0:T(8,128)S(1)}, u32[]{:S(2)}, u32[]{:S(2)}) collective-permute-start(f32[256,256]{1,0:T(8,128)S(1)} %mix.99.mine_ref), channel_id=1, source_target_pairs={{0,16},{1,17},{2,18},{3,19},{4,20},{5,21},{6,22},{7,23},{8,24},{9,... | collective-permute-start | bytes 786440 | tf_op jit(solution)/shard_map/ppermute | solution.py:91
  119.8 0.5 collective-permute-start.19
  120.5 0.5 collective-permute-done.14.got_ref
  121.3 3.3 %collective-permute-start.18 = (f32[256,128]{1,0:T(8,128)S(1)}, f32[256,128]{1,0:T(8,128)S(1)}, u32[]{:S(2)}, u32[]{:S(2)}) collective-permute-start(f32[256,128]{1,0:T(8,128)S(1)} %mix.101.mine_ref), channel_id=1, source_target_pairs={{0,8},{1,9},{2,10},{3,11},{4,12},{5,13},{6,14},{7,15},{8,0},{9,1},... | collective-permute-start | bytes 393224 | tf_op jit(solution)/shard_map/ppermute | solution.py:91
  124.6 0.4 mix.102.own_ref
  125.0 0.4 mix.103.mine_ref
  125.4 2.7 %collective-permute-start.17 = (f32[256,384]{1,0:T(8,128)S(1)}, f32[256,384]{1,0:T(8,128)S(1)}, u32[]{:S(2)}, u32[]{:S(2)}) collective-permute-start(f32[256,384]{1,0:T(8,128)S(1)} %mix.103.mine_ref), channel_id=1, source_target_pairs={{0,128},{1,129},{2,130},{3,131},{4,132},{5,133},{6,134},{7,135},{8... | collective-permute-start | bytes 1179656 | tf_op jit(solution)/shard_map/ppermute | solution.py:91
  128.6 0.7 collective-permute-start.23
  130.1 2.6 %collective-permute-done.18.got_ref = f32[256,128]{1,0:T(8,128)S(1)} collective-permute-done((f32[256,128]{1,0:T(8,128)S(1)}, f32[256,128]{1,0:T(8,128)S(1)}, u32[]{:S(2)}, u32[]{:S(2)}) %collective-permute-start.18) | collective-permute-done | bytes 131104 | tf_op jit(solution)/shard_map/ppermute | solution.py:91
  132.9 3.1 %collective-permute-start.22 = (f32[256,128]{1,0:T(8,128)S(1)}, f32[256,128]{1,0:T(8,128)S(1)}, u32[]{:S(2)}, u32[]{:S(2)}) collective-permute-start(f32[256,128]{1,0:T(8,128)S(1)} %mix.109.mine_ref), channel_id=1, source_target_pairs={{0,16},{1,17},{2,18},{3,19},{4,20},{5,21},{6,22},{7,23},{8,24},{9,... | collective-permute-start | bytes 393224 | tf_op jit(solution)/shard_map/ppermute | solution.py:91
  136.0 2.3 %collective-permute-start.21 = (f32[256,256]{1,0:T(8,128)S(1)}, f32[256,256]{1,0:T(8,128)S(1)}, u32[]{:S(2)}, u32[]{:S(2)}) collective-permute-start(f32[256,256]{1,0:T(8,128)S(1)} %mix.107.mine_ref), channel_id=1, source_target_pairs={{0,128},{1,129},{2,130},{3,131},{4,132},{5,133},{6,134},{7,135},{8... | collective-permute-start | bytes 786440 | tf_op jit(solution)/shard_map/ppermute | solution.py:91
  138.3 0.4 mix.110.own_ref
  138.7 0.4 mix.111
  139.9 0.5 collective-permute-done.22.got_ref
  140.6 1.2 collective-permute-start.24
  141.8 0.5 collective-permute-start.25
  142.5 3.2 %collective-permute-done.24.got_ref = f32[256,128]{1,0:T(8,128)S(1)} collective-permute-done((f32[256,128]{1,0:T(8,128)S(1)}, f32[256,128]{1,0:T(8,128)S(1)}, u32[]{:S(2)}, u32[]{:S(2)}) %collective-permute-start.24) | collective-permute-done | bytes 131104 | tf_op jit(solution)/shard_map/ppermute | solution.py:91
  146.0 1.4 collective-permute-start.27
  148.2 4.3 %collective-permute-done.25.got_ref = f32[256,256]{1,0:T(8,128)S(1)} collective-permute-done((f32[256,256]{1,0:T(8,128)S(1)}, f32[256,256]{1,0:T(8,128)S(1)}, u32[]{:S(2)}, u32[]{:S(2)}) %collective-permute-start.25) | collective-permute-done | bytes 262176 | tf_op jit(solution)/shard_map/ppermute | solution.py:91
  153.2 1.2 collective-permute-done.27.got_ref
  154.6 2.3 %collective-permute-start.28 = (f32[256,128]{1,0:T(8,128)S(1)}, f32[256,128]{1,0:T(8,128)S(1)}, u32[]{:S(2)}, u32[]{:S(2)}) collective-permute-start(f32[256,128]{1,0:T(8,128)S(1)} %mix.123.mine_ref), channel_id=1, source_target_pairs={{0,128},{1,129},{2,130},{3,131},{4,132},{5,133},{6,134},{7,135},{8... | collective-permute-start | bytes 393224 | tf_op jit(solution)/shard_map/ppermute | solution.py:91
  157.2 4.3 %collective-permute-done.26.got_ref = f32[256,256]{1,0:T(8,128)S(1)} collective-permute-done((f32[256,256]{1,0:T(8,128)S(1)}, f32[256,256]{1,0:T(8,128)S(1)}, u32[]{:S(2)}, u32[]{:S(2)}) %collective-permute-start.26) | collective-permute-done | bytes 262176 | tf_op jit(solution)/shard_map/ppermute | solution.py:91
  162.1 0.9 collective-permute-done.28.got_ref
  163.2 1.1 pad_maximum_fusion
  (67 shorter events, 12.4 us)
Async XLA Ops:
  0.0 4.4 %collective-permute-start = (f32[256,1024]{1,0:T(8,128)}, f32[256,1024]{1,0:T(8,128)S(1)}, u32[]{:S(2)}, u32[]{:S(2)}) collective-permute-start(f32[256,1024]{1,0:T(8,128)} %mine_ref.4), channel_id=1, source_target_pairs={{0,1},{1,0},{2,3},{3,2},{4,5},{5,4},{6,7},{7,6},{8,9},{9,8},{10,11... | collective-permute-start | bytes 3145736 | tf_op jit(solution)/shard_map/ppermute | solution.py:91
  0.0 2.2 %copy-start = (f32[8,256,512]{2,1,0:T(8,128)S(1)}, f32[8,256,512]{2,1,0:T(8,128)}, u32[]{:S(2)}) copy-start(f32[8,256,512]{2,1,0:T(8,128)} %matrix_ref.3) | copy-start | bytes 12582916
  2.2 0.7 copy-start.1
  2.8 1.2 copy-start.2
  4.8 11.8 %collective-permute-start.1 = (f32[256,384]{1,0:T(8,128)S(1)}, f32[256,384]{1,0:T(8,128)S(1)}, u32[]{:S(2)}, u32[]{:S(2)}) collective-permute-start(f32[256,384]{1,0:T(8,128)S(1)} %mix.65.mine_ref), channel_id=1, source_target_pairs={{0,2},{1,3},{2,0},{3,1},{4,6},{5,7},{6,4},{7,5},{8,10},{9,11},{10,... | collective-permute-start | bytes 1179656 | tf_op jit(solution)/shard_map/ppermute | solution.py:91
  17.0 20.9 %collective-permute-start.2 = (f32[256,384]{1,0:T(8,128)S(1)}, f32[256,384]{1,0:T(8,128)S(1)}, u32[]{:S(2)}, u32[]{:S(2)}) collective-permute-start(f32[256,384]{1,0:T(8,128)S(1)} %mix.67.mine_ref), channel_id=1, source_target_pairs={{0,4},{1,5},{2,6},{3,7},{4,0},{5,1},{6,2},{7,3},{8,12},{9,13},{10,... | collective-permute-start | bytes 1179656 | tf_op jit(solution)/shard_map/ppermute | solution.py:91
  20.9 17.6 %collective-permute-start.4 = (f32[256,256]{1,0:T(8,128)S(1)}, f32[256,256]{1,0:T(8,128)S(1)}, u32[]{:S(2)}, u32[]{:S(2)}) collective-permute-start(f32[256,256]{1,0:T(8,128)S(1)} %mix.69.mine_ref), channel_id=1, source_target_pairs={{0,2},{1,3},{2,0},{3,1},{4,6},{5,7},{6,4},{7,5},{8,10},{9,11},{10,... | collective-permute-start | bytes 786440 | tf_op jit(solution)/shard_map/ppermute | solution.py:91
  38.8 30.9 %collective-permute-start.5 = (f32[256,256]{1,0:T(8,128)S(1)}, f32[256,256]{1,0:T(8,128)S(1)}, u32[]{:S(2)}, u32[]{:S(2)}) collective-permute-start(f32[256,256]{1,0:T(8,128)S(1)} %mix.73.mine_ref), channel_id=1, source_target_pairs={{0,4},{1,5},{2,6},{3,7},{4,0},{5,1},{6,2},{7,3},{8,12},{9,13},{10,... | collective-permute-start | bytes 786440 | tf_op jit(solution)/shard_map/ppermute | solution.py:91
  38.9 37.5 %collective-permute-start.3 = (f32[256,384]{1,0:T(8,128)S(1)}, f32[256,384]{1,0:T(8,128)S(1)}, u32[]{:S(2)}, u32[]{:S(2)}) collective-permute-start(f32[256,384]{1,0:T(8,128)S(1)} %mix.71.mine_ref), channel_id=1, source_target_pairs={{0,8},{1,9},{2,10},{3,11},{4,12},{5,13},{6,14},{7,15},{8,0},{9,1},... | collective-permute-start | bytes 1179656 | tf_op jit(solution)/shard_map/ppermute | solution.py:91
  45.8 34.3 %collective-permute-start.7 = (f32[256,256]{1,0:T(8,128)S(1)}, f32[256,256]{1,0:T(8,128)S(1)}, u32[]{:S(2)}, u32[]{:S(2)}) collective-permute-start(f32[256,256]{1,0:T(8,128)S(1)} %mix.75.mine_ref), channel_id=1, source_target_pairs={{0,2},{1,3},{2,0},{3,1},{4,6},{5,7},{6,4},{7,5},{8,10},{9,11},{10,... | collective-permute-start | bytes 786440 | tf_op jit(solution)/shard_map/ppermute | solution.py:91
  48.8 45.1 %collective-permute-start.12 = (f32[256,128]{1,0:T(8,128)S(1)}, f32[256,128]{1,0:T(8,128)S(1)}, u32[]{:S(2)}, u32[]{:S(2)}) collective-permute-start(f32[256,128]{1,0:T(8,128)S(1)} %mix.77.mine_ref), channel_id=1, source_target_pairs={{0,2},{1,3},{2,0},{3,1},{4,6},{5,7},{6,4},{7,5},{8,10},{9,11},{10,... | collective-permute-start | bytes 393224 | tf_op jit(solution)/shard_map/ppermute | solution.py:91
  70.0 19.7 %collective-permute-start.9 = (f32[256,256]{1,0:T(8,128)S(1)}, f32[256,256]{1,0:T(8,128)S(1)}, u32[]{:S(2)}, u32[]{:S(2)}) collective-permute-start(f32[256,256]{1,0:T(8,128)S(1)} %mix.79.mine_ref), channel_id=1, source_target_pairs={{0,8},{1,9},{2,10},{3,11},{4,12},{5,13},{6,14},{7,15},{8,0},{9,1},... | collective-permute-start | bytes 786440 | tf_op jit(solution)/shard_map/ppermute | solution.py:91
  76.8 12.3 %collective-permute-start.6 = (f32[256,384]{1,0:T(8,128)S(1)}, f32[256,384]{1,0:T(8,128)S(1)}, u32[]{:S(2)}, u32[]{:S(2)}) collective-permute-start(f32[256,384]{1,0:T(8,128)S(1)} %mix.81.mine_ref), channel_id=1, source_target_pairs={{0,16},{1,17},{2,18},{3,19},{4,20},{5,21},{6,22},{7,23},{8,24},{9,... | collective-permute-start | bytes 1179656 | tf_op jit(solution)/shard_map/ppermute | solution.py:91
  80.4 19.7 %collective-permute-start.11 = (f32[256,256]{1,0:T(8,128)S(1)}, f32[256,256]{1,0:T(8,128)S(1)}, u32[]{:S(2)}, u32[]{:S(2)}) collective-permute-start(f32[256,256]{1,0:T(8,128)S(1)} %mix.83.mine_ref), channel_id=1, source_target_pairs={{0,4},{1,5},{2,6},{3,7},{4,0},{5,1},{6,2},{7,3},{8,12},{9,13},{10,... | collective-permute-start | bytes 786440 | tf_op jit(solution)/shard_map/ppermute | solution.py:91
  90.0 11.6 %collective-permute-start.10 = (f32[256,256]{1,0:T(8,128)S(1)}, f32[256,256]{1,0:T(8,128)S(1)}, u32[]{:S(2)}, u32[]{:S(2)}) collective-permute-start(f32[256,256]{1,0:T(8,128)S(1)} %mix.87.mine_ref), channel_id=1, source_target_pairs={{0,16},{1,17},{2,18},{3,19},{4,20},{5,21},{6,22},{7,23},{8,24},{9,... | collective-permute-start | bytes 786440 | tf_op jit(solution)/shard_map/ppermute | solution.py:91
  93.1 16.2 %collective-permute-start.8 = (f32[256,384]{1,0:T(8,128)S(1)}, f32[256,384]{1,0:T(8,128)S(1)}, u32[]{:S(2)}, u32[]{:S(2)}) collective-permute-start(f32[256,384]{1,0:T(8,128)S(1)} %mix.85.mine_ref), channel_id=1, source_target_pairs={{0,32},{1,33},{2,34},{3,35},{4,36},{5,37},{6,38},{7,39},{8,40},{9,... | collective-permute-start | bytes 1179656 | tf_op jit(solution)/shard_map/ppermute | solution.py:91
  100.4 16.0 %collective-permute-start.15 = (f32[256,256]{1,0:T(8,128)S(1)}, f32[256,256]{1,0:T(8,128)S(1)}, u32[]{:S(2)}, u32[]{:S(2)}) collective-permute-start(f32[256,256]{1,0:T(8,128)S(1)} %mix.91.mine_ref), channel_id=1, source_target_pairs={{0,8},{1,9},{2,10},{3,11},{4,12},{5,13},{6,14},{7,15},{8,0},{9,1},... | collective-permute-start | bytes 786440 | tf_op jit(solution)/shard_map/ppermute | solution.py:91
  101.3 19.7 %collective-permute-start.14 = (f32[256,128]{1,0:T(8,128)S(1)}, f32[256,128]{1,0:T(8,128)S(1)}, u32[]{:S(2)}, u32[]{:S(2)}) collective-permute-start(f32[256,128]{1,0:T(8,128)S(1)} %mix.89.mine_ref), channel_id=1, source_target_pairs={{0,4},{1,5},{2,6},{3,7},{4,0},{5,1},{6,2},{7,3},{8,12},{9,13},{10,... | collective-permute-start | bytes 393224 | tf_op jit(solution)/shard_map/ppermute | solution.py:91
  101.9 10.8 %collective-permute-start.16 = (f32[256,256]{1,0:T(8,128)S(1)}, f32[256,256]{1,0:T(8,128)S(1)}, u32[]{:S(2)}, u32[]{:S(2)}) collective-permute-start(f32[256,256]{1,0:T(8,128)S(1)} %mix.93.mine_ref), channel_id=1, source_target_pairs={{0,32},{1,33},{2,34},{3,35},{4,36},{5,37},{6,38},{7,39},{8,40},{9,... | collective-permute-start | bytes 786440 | tf_op jit(solution)/shard_map/ppermute | solution.py:91
  109.7 15.3 %collective-permute-start.13 = (f32[256,384]{1,0:T(8,128)S(1)}, f32[256,384]{1,0:T(8,128)S(1)}, u32[]{:S(2)}, u32[]{:S(2)}) collective-permute-start(f32[256,384]{1,0:T(8,128)S(1)} %mix.95.mine_ref), channel_id=1, source_target_pairs={{0,64},{1,65},{2,66},{3,67},{4,68},{5,69},{6,70},{7,71},{8,72},{9,... | collective-permute-start | bytes 1179656 | tf_op jit(solution)/shard_map/ppermute | solution.py:91
  116.7 11.6 %collective-permute-start.20 = (f32[256,256]{1,0:T(8,128)S(1)}, f32[256,256]{1,0:T(8,128)S(1)}, u32[]{:S(2)}, u32[]{:S(2)}) collective-permute-start(f32[256,256]{1,0:T(8,128)S(1)} %mix.99.mine_ref), channel_id=1, source_target_pairs={{0,16},{1,17},{2,18},{3,19},{4,20},{5,21},{6,22},{7,23},{8,24},{9,... | collective-permute-start | bytes 786440 | tf_op jit(solution)/shard_map/ppermute | solution.py:91
  119.8 9.7 %collective-permute-start.19 = (f32[256,256]{1,0:T(8,128)S(1)}, f32[256,256]{1,0:T(8,128)S(1)}, u32[]{:S(2)}, u32[]{:S(2)}) collective-permute-start(f32[256,256]{1,0:T(8,128)S(1)} %mix.97.mine_ref), channel_id=1, source_target_pairs={{0,64},{1,65},{2,66},{3,67},{4,68},{5,69},{6,70},{7,71},{8,72},{9,... | collective-permute-start | bytes 786440 | tf_op jit(solution)/shard_map/ppermute | solution.py:91
  121.3 11.4 %collective-permute-start.18 = (f32[256,128]{1,0:T(8,128)S(1)}, f32[256,128]{1,0:T(8,128)S(1)}, u32[]{:S(2)}, u32[]{:S(2)}) collective-permute-start(f32[256,128]{1,0:T(8,128)S(1)} %mix.101.mine_ref), channel_id=1, source_target_pairs={{0,8},{1,9},{2,10},{3,11},{4,12},{5,13},{6,14},{7,15},{8,0},{9,1},... | collective-permute-start | bytes 393224 | tf_op jit(solution)/shard_map/ppermute | solution.py:91
  125.4 13.3 %collective-permute-start.17 = (f32[256,384]{1,0:T(8,128)S(1)}, f32[256,384]{1,0:T(8,128)S(1)}, u32[]{:S(2)}, u32[]{:S(2)}) collective-permute-start(f32[256,384]{1,0:T(8,128)S(1)} %mix.103.mine_ref), channel_id=1, source_target_pairs={{0,128},{1,129},{2,130},{3,131},{4,132},{5,133},{6,134},{7,135},{8... | collective-permute-start | bytes 1179656 | tf_op jit(solution)/shard_map/ppermute | solution.py:91
  128.6 10.8 %collective-permute-start.23 = (f32[256,256]{1,0:T(8,128)S(1)}, f32[256,256]{1,0:T(8,128)S(1)}, u32[]{:S(2)}, u32[]{:S(2)}) collective-permute-start(f32[256,256]{1,0:T(8,128)S(1)} %mix.105.mine_ref), channel_id=1, source_target_pairs={{0,32},{1,33},{2,34},{3,35},{4,36},{5,37},{6,38},{7,39},{8,40},{9,... | collective-permute-start | bytes 786440 | tf_op jit(solution)/shard_map/ppermute | solution.py:91
  132.9 7.4 %collective-permute-start.22 = (f32[256,128]{1,0:T(8,128)S(1)}, f32[256,128]{1,0:T(8,128)S(1)}, u32[]{:S(2)}, u32[]{:S(2)}) collective-permute-start(f32[256,128]{1,0:T(8,128)S(1)} %mix.109.mine_ref), channel_id=1, source_target_pairs={{0,16},{1,17},{2,18},{3,19},{4,20},{5,21},{6,22},{7,23},{8,24},{9,... | collective-permute-start | bytes 393224 | tf_op jit(solution)/shard_map/ppermute | solution.py:91
  136.0 11.6 %collective-permute-start.21 = (f32[256,256]{1,0:T(8,128)S(1)}, f32[256,256]{1,0:T(8,128)S(1)}, u32[]{:S(2)}, u32[]{:S(2)}) collective-permute-start(f32[256,256]{1,0:T(8,128)S(1)} %mix.107.mine_ref), channel_id=1, source_target_pairs={{0,128},{1,129},{2,130},{3,131},{4,132},{5,133},{6,134},{7,135},{8... | collective-permute-start | bytes 786440 | tf_op jit(solution)/shard_map/ppermute | solution.py:91
  140.6 5.1 %collective-permute-start.24 = (f32[256,128]{1,0:T(8,128)S(1)}, f32[256,128]{1,0:T(8,128)S(1)}, u32[]{:S(2)}, u32[]{:S(2)}) collective-permute-start(f32[256,128]{1,0:T(8,128)S(1)} %mix.115.mine_ref), channel_id=1, source_target_pairs={{0,32},{1,33},{2,34},{3,35},{4,36},{5,37},{6,38},{7,39},{8,40},{9,... | collective-permute-start | bytes 393224 | tf_op jit(solution)/shard_map/ppermute | solution.py:91
  141.8 10.7 %collective-permute-start.25 = (f32[256,256]{1,0:T(8,128)S(1)}, f32[256,256]{1,0:T(8,128)S(1)}, u32[]{:S(2)}, u32[]{:S(2)}) collective-permute-start(f32[256,256]{1,0:T(8,128)S(1)} %mix.113.mine_ref), channel_id=1, source_target_pairs={{0,64},{1,65},{2,66},{3,67},{4,68},{5,69},{6,70},{7,71},{8,72},{9,... | collective-permute-start | bytes 786440 | tf_op jit(solution)/shard_map/ppermute | solution.py:91
  146.0 8.4 %collective-permute-start.27 = (f32[256,128]{1,0:T(8,128)S(1)}, f32[256,128]{1,0:T(8,128)S(1)}, u32[]{:S(2)}, u32[]{:S(2)}) collective-permute-start(f32[256,128]{1,0:T(8,128)S(1)} %mix.117.mine_ref), channel_id=1, source_target_pairs={{0,64},{1,65},{2,66},{3,67},{4,68},{5,69},{6,70},{7,71},{8,72},{9,... | collective-permute-start | bytes 393224 | tf_op jit(solution)/shard_map/ppermute | solution.py:91
  152.7 8.8 %collective-permute-start.26 = (f32[256,256]{1,0:T(8,128)S(1)}, f32[256,256]{1,0:T(8,128)S(1)}, u32[]{:S(2)}, u32[]{:S(2)}) collective-permute-start(f32[256,256]{1,0:T(8,128)S(1)} %mix.121.mine_ref), channel_id=1, source_target_pairs={{0,128},{1,129},{2,130},{3,131},{4,132},{5,133},{6,134},{7,135},{8... | collective-permute-start | bytes 786440 | tf_op jit(solution)/shard_map/ppermute | solution.py:91
  154.6 8.3 %collective-permute-start.28 = (f32[256,128]{1,0:T(8,128)S(1)}, f32[256,128]{1,0:T(8,128)S(1)}, u32[]{:S(2)}, u32[]{:S(2)}) collective-permute-start(f32[256,128]{1,0:T(8,128)S(1)} %mix.123.mine_ref), channel_id=1, source_target_pairs={{0,128},{1,129},{2,130},{3,131},{4,132},{5,133},{6,134},{7,135},{8... | collective-permute-start | bytes 393224 | tf_op jit(solution)/shard_map/ppermute | solution.py:91
